TPU v7x, 512 devices: a whole 4x4x16 slice. The times are simulated.
512 devices in a mesh: slide: 128 (over x, z, core), rep: 4 (over y).
Axes of the slice: x: 4, y: 4, z: 16, core: 2. Of those that a mesh axis runs over, the one named last changes fastest.
Arguments:
- tile_feats: bfloat16 [2048, 8, 8, 192], P(('slide', 'rep'))
- cotangent: bfloat16 [2048, 4, 4, 384], P(('slide', 'rep')), may hold values from -0.03125 to 0.03125
- keep_list: int32 [512, 4], P(('slide', 'rep')), may hold values from 0 to 3, each once within a row
- tile_plan: int32 [512, 2], P(('slide', 'rep')), may hold values from 0 to 4, as said below
- kernel_one: bfloat16 [7, 7, 192], replicated, may hold values from -0.875 to 0.875
- gain_one: bfloat16 [192], replicated, may hold values from 0.25 to 1.75
- inward_one: bfloat16 [192, 768], replicated, may hold values from -0.4375 to 0.4375
- outward_one: bfloat16 [768, 192], replicated, may hold values from -0.21875 to 0.21875
- gain_down: bfloat16 [192], replicated, may hold values from 0.25 to 1.75
- project_down: bfloat16 [768, 384], replicated, may hold values from -0.21875 to 0.21875
- kernel_two: bfloat16 [7, 7, 384], replicated, may hold values from -0.875 to 0.875
- gain_two: bfloat16 [384], replicated, may hold values from 0.25 to 1.75
- inward_two: bfloat16 [384, 1536], replicated, may hold values from -0.3125 to 0.3125
- outward_two: bfloat16 [1536, 384], replicated, may hold values from -0.15625 to 0.15625
Outputs:
- features: bfloat16 [2048, 4, 4, 384], P(('slide', 'rep'))
- grad_inward: float32 [192, 768], P(None, 'slide')
- grad_outward: float32 [768, 192], P('slide')
- grad_project: float32 [768, 384], P('slide')
Inputs may be any that keep to these rules, and one draw needn't show every extreme that they name: `keep_list`: each row is a permutation of 0 to 3. `tile_plan`: column 0 counts the device's kept tiles, column 1 is its partner bit, from 0 to 2. The device at the same rep index whose slide index differs only in that bit is its partner and has the same partner bit; the bit is the same over each aligned group of 8 slide indices. Partners' counts sum to at most 4. In every replica some device keeps 4 tiles and its partner none.
All inputs are finite; a program needn't handle non-finite values.
Results may differ from a plain program's by a relative error of at most 0.018.
Values may be sent and summed in bfloat16 or wider, within the bound.
No kernel may reach another device: no remote copies, remote signals or barrier semaphores. Data moves between devices by JAX's collectives and lax.ppermute only.
A program may use at most 64 MiB of HBM per device.

v0:
```python
import jax
import jax.numpy as jnp
from jax import lax
from jax.sharding import Mesh
from jax.sharding import PartitionSpec as P

SLIDE = ("slide_0", "slide_1", "slide_2")
SLIDE_REP = ("slide_0", "slide_1", "slide_2", "rep")


def split_up(shard, dim, size):
    lengths = shard.shape
    pieces = shard.reshape(*lengths[:dim], size, lengths[dim] // size, *lengths[dim + 1 :])
    return jnp.moveaxis(pieces, dim, 0)


def summed_on_arrival(shard, axis, dim):
    pieces = split_up(shard, dim, lax.axis_size(axis))
    arrived = lax.all_to_all(pieces, axis, split_axis=0, concat_axis=0, tiled=True)
    return arrived.sum(axis=0)


def sum_in_two_steps(shard, axes, dim):
    far, near = axes
    pieces = split_up(shard, dim, lax.axis_size(far))
    nearer = summed_on_arrival(pieces, near, dim + 1)
    arrived = lax.all_to_all(nearer, far, split_axis=0, concat_axis=0, tiled=True)
    return arrived.sum(axis=0)


def in_one_piece(arrays, axis, dim, along):
    widths = [a.shape[along] for a in arrays]
    both = jnp.concatenate(arrays, axis=along)
    whole = sum_in_two_steps(both, axis, dim)
    return tuple(jnp.split(whole, [sum(widths[:k]) for k in range(1, len(widths))], axis=along))


def sent_to_all(shard, axis):
    copies = jnp.broadcast_to(shard, (lax.axis_size(axis), *shard.shape))
    return lax.all_to_all(copies, axis, split_axis=0, concat_axis=0, tiled=True)


def over_copies(shard, axis):
    return sent_to_all(shard, axis).sum(axis=0)


def together(arrays, axis):
    ends = [0]
    for a in arrays:
        ends.append(ends[-1] + a.size)
    total = over_copies(jnp.concatenate([a.ravel() for a in arrays]), axis)
    return tuple((total[b:e].reshape(a.shape) for a, b, e in zip(arrays, ends, ends[1:])))


def depthwise(field, kernel):
    return lax.conv_general_dilated(
        field.astype(jnp.float32),
        kernel.astype(jnp.float32)[:, :, None, :],
        (1, 1),
        "SAME",
        dimension_numbers=("NHWC", "HWIO", "NHWC"),
        feature_group_count=field.shape[-1],
        precision=lax.Precision.HIGHEST,
    )


def layer_norm(values, gain):
    centre = jnp.mean(values, axis=-1, keepdims=True)
    offset = values - centre
    spread = jnp.mean(offset * offset, axis=-1, keepdims=True)
    return offset * lax.rsqrt(spread + 1e-06) * gain.astype(jnp.float32)


def gelu_exact(values):
    return jax.nn.gelu(values, approximate=False)


def slot_pass(tile_feats, cotangent, weights):
    (
        kernel_one,
        gain_one,
        inward_one,
        outward_one,
        gain_down,
        project_down,
        kernel_two,
        gain_two,
        inward_two,
        outward_two,
    ) = weights
    slot_count = tile_feats.shape[0]
    side_cells = tile_feats.shape[1]
    narrow_width = tile_feats.shape[3]
    half_side = side_cells // 2
    wide_width = project_down.shape[1]
    first_rows = slot_count * side_cells * side_cells
    second_rows = slot_count * half_side * half_side
    normed = (
        layer_norm(depthwise(tile_feats, kernel_one), gain_one)
        .astype(jnp.bfloat16)
        .reshape(first_rows, narrow_width)
    )
    expand = jnp.dot(normed, inward_one, preferred_element_type=jnp.float32)
    hidden = gelu_exact(expand).astype(jnp.bfloat16)
    flat_input = tile_feats.reshape(first_rows, narrow_width)
    section_one = (
        flat_input.astype(jnp.float32)
        + jnp.dot(hidden, outward_one, preferred_element_type=jnp.float32)
    ).astype(jnp.bfloat16)
    down_normed = layer_norm(section_one.astype(jnp.float32), gain_down).astype(jnp.bfloat16)
    patches = (
        down_normed.reshape(slot_count, half_side, 2, half_side, 2, narrow_width)
        .transpose(0, 1, 3, 2, 4, 5)
        .reshape(second_rows, 4 * narrow_width)
    )
    merged = jnp.dot(patches, project_down, preferred_element_type=jnp.float32).astype(jnp.bfloat16)
    merged_grid = merged.reshape(slot_count, half_side, half_side, wide_width).astype(jnp.float32)

    def second_norm(values):
        return layer_norm(depthwise(values, kernel_two), gain_two)

    normed_two = second_norm(merged_grid).astype(jnp.bfloat16).reshape(second_rows, wide_width)
    expand_two = jnp.dot(normed_two, inward_two, preferred_element_type=jnp.float32)
    hidden_two = gelu_exact(expand_two).astype(jnp.bfloat16)
    features = (
        merged.astype(jnp.float32)
        + jnp.dot(hidden_two, outward_two, preferred_element_type=jnp.float32)
    ).astype(jnp.bfloat16)
    flat_cot = cotangent.reshape(second_rows, wide_width)
    back_hidden_two = jnp.dot(flat_cot, outward_two.T, preferred_element_type=jnp.float32).astype(
        jnp.bfloat16
    )
    unused, gelu_back_two = jax.vjp(gelu_exact, expand_two)
    back_expand_two = gelu_back_two(back_hidden_two.astype(jnp.float32))[0].astype(jnp.bfloat16)
    back_normed_two = jnp.dot(
        back_expand_two, inward_two.T, preferred_element_type=jnp.float32
    ).astype(jnp.bfloat16)
    unused, norm_back_two = jax.vjp(second_norm, merged_grid)
    back_depth = norm_back_two(
        back_normed_two.astype(jnp.float32).reshape(slot_count, half_side, half_side, wide_width)
    )[0]
    back_merged = (
        flat_cot.astype(jnp.float32) + back_depth.reshape(second_rows, wide_width)
    ).astype(jnp.bfloat16)
    grad_project = jnp.dot(patches.T, back_merged, preferred_element_type=jnp.float32)
    back_patches = jnp.dot(back_merged, project_down.T, preferred_element_type=jnp.float32).astype(
        jnp.bfloat16
    )
    back_down = (
        back_patches.reshape(slot_count, half_side, half_side, 2, 2, narrow_width)
        .transpose(0, 1, 3, 2, 4, 5)
        .reshape(first_rows, narrow_width)
    )
    unused, norm_back_down = jax.vjp(
        lambda values: layer_norm(values, gain_down), section_one.astype(jnp.float32)
    )
    back_section = norm_back_down(back_down.astype(jnp.float32))[0].astype(jnp.bfloat16)
    grad_outward = jnp.dot(hidden.T, back_section, preferred_element_type=jnp.float32)
    back_hidden = jnp.dot(back_section, outward_one.T, preferred_element_type=jnp.float32).astype(
        jnp.bfloat16
    )
    unused, gelu_back = jax.vjp(gelu_exact, expand)
    back_expand = gelu_back(back_hidden.astype(jnp.float32))[0].astype(jnp.bfloat16)
    grad_inward = jnp.dot(normed.T, back_expand, preferred_element_type=jnp.float32)
    return (
        features.reshape(slot_count, half_side, half_side, wide_width),
        grad_inward,
        grad_outward,
        grad_project,
    )


def column_mask(mask, rank):
    return mask.reshape(mask.shape + (1,) * rank)


def per_device(
    tile_feats,
    cotangent,
    keep_list,
    tile_plan,
    kernel_one,
    gain_one,
    inward_one,
    outward_one,
    gain_down,
    project_down,
    kernel_two,
    gain_two,
    inward_two,
    outward_two,
):
    weights = (
        kernel_one,
        gain_one,
        inward_one,
        outward_one,
        gain_down,
        project_down,
        kernel_two,
        gain_two,
        inward_two,
        outward_two,
    )
    candidates = tile_feats.shape[0]
    ordering = keep_list[0]
    kept_count = tile_plan[0, 0]
    positions = jnp.arange(candidates, dtype=jnp.int32)
    live = positions < kept_count
    zero_value = jnp.zeros((), jnp.bfloat16)
    ordered_tiles = jnp.where(column_mask(live, 3), tile_feats[ordering], zero_value)
    ordered_cot = jnp.where(column_mask(live, 3), cotangent[ordering], zero_value)
    position_feats, grad_inward, grad_outward, grad_project = slot_pass(
        ordered_tiles, ordered_cot, weights
    )
    place = jnp.sum(
        jnp.where(ordering[None, :] == positions[:, None], positions[None, :], 0), axis=1
    )
    features = jnp.where(column_mask(place < kept_count, 3), position_feats[place], zero_value)
    shares = (
        sum_in_two_steps(grad_inward, (("slide_0", "slide_1"), "slide_2"), 1),
        *in_one_piece((grad_outward, grad_project), (("slide_0", "slide_1"), "slide_2"), 0, 1),
    )
    summed = together((shares[0], shares[1], shares[2]), "rep")
    inward_share = summed[0]
    outward_share = summed[1]
    project_share = summed[2]
    return (features, inward_share, outward_share, project_share)


def solution(mesh):
    split = Mesh(
        mesh.devices.reshape(4, 16, 2, mesh.shape["rep"]), ("slide_0", "slide_1", "slide_2", "rep")
    )
    return jax.shard_map(
        per_device,
        mesh=split,
        in_specs=(
            P(SLIDE_REP, None, None, None),
            P(SLIDE_REP, None, None, None),
            P(SLIDE_REP, None),
            P(SLIDE_REP, None),
            P(),
            P(),
            P(),
            P(),
            P(),
            P(),
            P(),
            P(),
            P(),
            P(),
        ),
        out_specs=(P(SLIDE_REP, None, None, None), P(None, SLIDE), P(SLIDE, None), P(SLIDE, None)),
        check_vma=False,
    )
```

profile of v0, /device:TPU:6, one launch (start us, length us, event | category | flops | bytes accessed | tf_op | source)
XLA Modules:
  0.0 182.2 jit_solution(11987014508865246036)
XLA Ops:
  0.6 0.8 fusion.66
  1.4 0.8 select_reduce_fusion
  2.2 0.7 convert_element_type.117
  2.8 0.7 convert_element_type.112
  3.5 0.7 convert_element_type.121
  4.2 0.6 iota_compare_fusion.1
  5.2 1.4 gather_fusion.2
  6.6 1.5 gather_fusion
  8.3 2.2 %fusion.80 = (f32[4,8,8]{0,2,1:T(8,128)S(1)}, f32[4,8,8,192]{3,0,2,1:T(4,128)S(1)}) fusion(bf16[7,7,1,192]{3,1,0,2:T(8,128)(2,1)} %bitcast.123, bf16[4,8,8,192]{3,2,1,0:T(8,128)(2,1)S(1)} %broadcast_select_fusion), kind=kOutput, calls=%fused_computation.152 | convolution fusion | flops 3022592 | bytes 314752 | tf_op jit(solution)/shard_map/conv_general_dilated | solution.py:56
  10.5 0.3 multiply_reduce_fusion
  11.1 2.6 %fusion.10 = (bf16[256,768]{1,0:T(8,128)(2,1)S(1)}, f32[256,768]{1,0:T(8,128)}) fusion(bf16[256,192]{1,0:T(8,128)(2,1)S(1)} %bitcast.117, bf16[192,768]{1,0:T(8,128)(2,1)S(1)} %copy-done.8), kind=kOutput, calls=%fused_computation.23 | convolution fusion | flops 88276992 | bytes 1572864 | tf_op jit(solution)/shard_map/dot_general | solution.py:103
  13.6 0.3 fusion.81
  15.0 0.6 fusion.82
  16.0 0.3 fusion.83
  16.4 2.7 %fusion.7 = f32[64,384]{1,0:T(8,128)S(1)} fusion(bf16[384,1536]{1,0:T(8,128)(2,1)S(1)} %copy-done, bf16[1536,384]{1,0:T(8,128)(2,1)} %param.27, f32[64,1536]{1,0:T(8,128)S(1)} %fusion.83, bf16[64,384]{1,0:T(8,128)(2,1)S(1)} %gather.17, pred[64]{0:T(512)(128)(4,1)S(1)} %broadcast_in_dim.116), kind=kOutput, calls=%fused_computation.19 | convolution fusion | flops 158343168 | bytes 2900032 | tf_op jit(solution)/shard_map/dot_general | solution.py:135
  19.6 0.6 add_convert_fusion.2
  20.3 0.3 fusion.5
  20.6 0.2 reshape.231
  21.5 0.3 copy-done.5
  21.8 3.1 %fusion.15 = bf16[768,256]{0,1:T(8,128)(2,1)S(1)} fusion(bf16[768,192]{0,1:T(8,128)(2,1)S(1)} %copy-done.5, f32[256,768]{1,0:T(8,128)} %get-tuple-element.39, f32[256,192]{0,1:T(8,128)S(1)} %get-tuple-element.33, f32[256]{0:T(256)S(1)} %negate_multiply_fusion.4), kind=kOutput, calls=%fused_computation.28 | convolution fusion | flops 90144768 | bytes 1672192 | tf_op jit(solution)/shard_map/dot_general | solution.py:159
  25.2 1.2 fusion.40
  26.4 4.5 %all-to-all-start = ((f32[2,64,192,6]{2,1,3,0:T(8,128)}), f32[2,64,192,6]{2,1,3,0:T(8,128)}, u32[]{:S(2)}, u32[]{:S(2)}) async-start(f32[2,64,192,6]{2,1,3,0:T(8,128)} %bitcast.19), calls=%async_computation | async-start | bytes 1572864 | tf_op jit(solution)/shard_map/all_to_all | solution.py:19
  30.9 0.2 fusion.63
  31.2 0.4 fusion.84
  31.5 1.3 pad_maximum_fusion
  32.9 1.9 %copy.177 = f32[768,576]{1,0:T(8,128)S(1)} copy(f32[768,576]{0,1:T(8,128)} %pad_maximum_fusion) | data formatting | bytes 3538944 | tf_op jit(solution)/shard_map/concatenate | solution.py:33
  34.7 1.7 reshape_reshape.3
  36.4 3.6 %copy.178 = f32[2,64,6,576]{3,1,2,0:T(8,128)} copy(f32[2,64,6,576]{3,2,0,1:T(8,128)} %bitcast.114) | data formatting | bytes 3538944 | tf_op jit(solution)/shard_map/transpose | solution.py:14
  40.0 3.7 %all-to-all-start.2 = ((f32[2,64,6,576]{3,1,2,0:T(8,128)}), f32[2,64,6,576]{3,1,2,0:T(8,128)S(1)}, u32[]{:S(2)}, u32[]{:S(2)}) async-start(f32[2,64,6,576]{3,1,2,0:T(8,128)} %copy.178), calls=%async_computation.2 | async-start | bytes 3932160 | tf_op jit(solution)/shard_map/all_to_all | solution.py:19
  43.8 1.2 reduce_sum.163
  45.0 1.0 copy.173
  46.0 0.5 all-to-all-done.2
  46.5 19.0 %all-to-all-start.1 = ((f32[64,192,6]{1,2,0:T(8,128)}), f32[64,192,6]{1,2,0:T(8,128)}, u32[]{:S(2)}, u32[]{:S(2)}) async-start(f32[64,192,6]{1,2,0:T(8,128)} %copy.173), calls=%async_computation.1 | async-start | bytes 1048576 | tf_op jit(solution)/shard_map/all_to_all | solution.py:27
  65.5 1.2 reduce_sum.192
  66.7 2.9 %copy.179 = f32[64,6,576]{2,1,0:T(8,128)} copy(f32[64,6,576]{2,0,1:T(8,128)} %reduce_sum.192) | data formatting | bytes 1769472 | tf_op jit(solution)/shard_map/reduce_sum | solution.py:20
  69.6 27.8 %all-to-all-done.1 = f32[64,192,6]{1,2,0:T(8,128)} async-done(((f32[64,192,6]{1,2,0:T(8,128)}), f32[64,192,6]{1,2,0:T(8,128)}, u32[]{:S(2)}, u32[]{:S(2)}) %all-to-all-start.1) | async-done | bytes 294944 | tf_op jit(solution)/shard_map/all_to_all | solution.py:27
  97.4 6.9 %all-to-all-start.3 = ((f32[64,6,576]{2,1,0:T(8,128)}), f32[64,6,576]{2,1,0:T(8,128)S(1)}, u32[]{:S(2)}, u32[]{:S(2)}) async-start(f32[64,6,576]{2,1,0:T(8,128)} %copy.179), calls=%async_computation.3 | async-start | bytes 2621440 | tf_op jit(solution)/shard_map/all_to_all | solution.py:27
  104.3 2.3 %fusion.6 = bf16[64,384]{1,0:T(8,128)(2,1)S(1)} fusion(bf16[1536,384]{1,0:T(8,128)(2,1)} %param.27, f32[64,1536]{1,0:T(8,128)S(1)} %copy-done.3, bf16[64,384]{1,0:T(8,128)(2,1)S(1)} %copy-done.7), kind=kOutput, calls=%fused_computation.17 | convolution fusion | flops 81960960 | bytes 1671168 | tf_op jit(solution)/shard_map/dot_general | solution.py:127
  106.6 0.6 gather_fusion.1
  107.2 1.1 reduce_sum.167
  108.6 60.3 %all-to-all-done.3 = f32[64,6,576]{2,1,0:T(8,128)S(1)} async-done(((f32[64,6,576]{2,1,0:T(8,128)}), f32[64,6,576]{2,1,0:T(8,128)S(1)}, u32[]{:S(2)}, u32[]{:S(2)}) %all-to-all-start.3) | async-done | bytes 884768 | tf_op jit(solution)/shard_map/all_to_all | solution.py:27
  169.2 0.7 broadcast_in_dim.125
  169.9 4.5 %all-to-all-start.4 = ((f32[4,1,4608]{2,1,0:T(1,128)}), f32[4,1,4608]{2,1,0:T(1,128)S(1)}, u32[]{:S(2)}, u32[]{:S(2)}) async-start(f32[4,1,4608]{2,1,0:T(1,128)} %broadcast_in_dim.125), calls=%async_computation.4 | async-start | bytes 147456 | tf_op jit(solution)/shard_map/all_to_all | solution.py:40
  174.5 0.6 copy.181
  175.1 4.9 %all-to-all-done.4 = f32[4,1,4608]{2,1,0:T(1,128)S(1)} async-done(((f32[4,1,4608]{2,1,0:T(1,128)}), f32[4,1,4608]{2,1,0:T(1,128)S(1)}, u32[]{:S(2)}, u32[]{:S(2)}) %all-to-all-start.4) | async-done | bytes 73760 | tf_op jit(solution)/shard_map/all_to_all | solution.py:40
  180.1 0.7 reshape.227
  180.8 0.6 slice.45
  181.6 0.7 copy.182
  (82 shorter events, 4.4 us)
Async XLA Ops:
  0.6 15.4 %copy-start = (bf16[384,1536]{1,0:T(8,128)(2,1)S(1)}, bf16[384,1536]{1,0:T(8,128)(2,1)}, u32[]{:S(2)}) copy-start(bf16[384,1536]{1,0:T(8,128)(2,1)} %param.26) | copy-start | bytes 3538948
  8.1 3.0 %copy-start.8 = (bf16[192,768]{1,0:T(8,128)(2,1)S(1)}, bf16[192,768]{1,0:T(8,128)(2,1)}, u32[]{:S(2)}) copy-start(bf16[192,768]{1,0:T(8,128)(2,1)} %param.20) | copy-start | bytes 884740
  11.1 2.6 %copy-start.4 = (bf16[768,192]{0,1:T(8,128)(2,1)S(1)}, bf16[768,192]{0,1:T(8,128)(2,1)}, u32[]{:S(2)}) copy-start(bf16[768,192]{0,1:T(8,128)(2,1)} %param.21) | copy-start | bytes 884740
  13.6 1.1 copy-start.1
  14.0 1.0 copy-start.9
  14.9 1.0 copy-start.6
  16.3 2.8 %copy-start.2 = (f32[64,1536]{1,0:T(8,128)}, f32[64,1536]{1,0:T(8,128)S(1)}, u32[]{:S(2)}) copy-start(f32[64,1536]{1,0:T(8,128)S(1)} %fusion.83) | copy-start | bytes 1179652
  20.9 1.0 copy-start.5
  26.4 13.6 %all-to-all-start = ((f32[2,64,192,6]{2,1,3,0:T(8,128)}), f32[2,64,192,6]{2,1,3,0:T(8,128)}, u32[]{:S(2)}, u32[]{:S(2)}) async-start(f32[2,64,192,6]{2,1,3,0:T(8,128)} %bitcast.19), calls=%async_computation | async-start | bytes 1572864 | tf_op jit(solution)/shard_map/all_to_all | solution.py:19
  40.0 6.5 %all-to-all-start.2 = ((f32[2,64,6,576]{3,1,2,0:T(8,128)}), f32[2,64,6,576]{3,1,2,0:T(8,128)S(1)}, u32[]{:S(2)}, u32[]{:S(2)}) async-start(f32[2,64,6,576]{3,1,2,0:T(8,128)} %copy.178), calls=%async_computation.2 | async-start | bytes 3932160 | tf_op jit(solution)/shard_map/all_to_all | solution.py:19
  46.5 50.9 %all-to-all-start.1 = ((f32[64,192,6]{1,2,0:T(8,128)}), f32[64,192,6]{1,2,0:T(8,128)}, u32[]{:S(2)}, u32[]{:S(2)}) async-start(f32[64,192,6]{1,2,0:T(8,128)} %copy.173), calls=%async_computation.1 | async-start | bytes 1048576 | tf_op jit(solution)/shard_map/all_to_all | solution.py:27
  69.6 34.7 %copy-start.3 = (f32[64,1536]{1,0:T(8,128)S(1)}, f32[64,1536]{1,0:T(8,128)}, u32[]{:S(2)}) copy-start(f32[64,1536]{1,0:T(8,128)} %copy-done.2) | copy-start | bytes 1179652
  69.6 34.7 %copy-start.7 = (bf16[64,384]{1,0:T(8,128)(2,1)S(1)}, bf16[64,384]{1,0:T(8,128)(2,1)}, u32[]{:S(2)}) copy-start(bf16[64,384]{1,0:T(8,128)(2,1)} %copy-done.6) | copy-start | bytes 147460
  97.4 71.6 %all-to-all-start.3 = ((f32[64,6,576]{2,1,0:T(8,128)}), f32[64,6,576]{2,1,0:T(8,128)S(1)}, u32[]{:S(2)}, u32[]{:S(2)}) async-start(f32[64,6,576]{2,1,0:T(8,128)} %copy.179), calls=%async_computation.3 | async-start | bytes 2621440 | tf_op jit(solution)/shard_map/all_to_all | solution.py:27
  169.9 10.1 %all-to-all-start.4 = ((f32[4,1,4608]{2,1,0:T(1,128)}), f32[4,1,4608]{2,1,0:T(1,128)S(1)}, u32[]{:S(2)}, u32[]{:S(2)}) async-start(f32[4,1,4608]{2,1,0:T(1,128)} %broadcast_in_dim.125), calls=%async_computation.4 | async-start | bytes 147456 | tf_op jit(solution)/shard_map/all_to_all | solution.py:40
where the time goes:
time: 183 us; the launch traced here: 182 us
  waiting for transfers between devices  93.6 us (51%)
  starting transfers between devices  38.6 us (21%)
  local copies, waits for them, and re-layouts  20.7 us (11%)
  matrix products  17.1 us (9%)
  other arithmetic  11.1 us (6%)
    all_to_all x2, waiting for transfers between devices, sum_in_two_steps(): lax.all_to_all(nearer, far, split_axis=0, concat_axis=0, tiled=True)  88.1 us
    all_to_all x2, starting transfers between devices, sum_in_two_steps(): lax.all_to_all(nearer, far, split_axis=0, concat_axis=0, tiled=True)  25.9 us
    all_to_all x2, starting transfers between devices, summed_on_arrival(): lax.all_to_all(pieces, axis, split_axis=0, concat_axis=0, tiled=True)  8.23 us
    all_to_all x1, waiting for transfers between devices, sent_to_all(): return lax.all_to_all(copies, axis, split_axis=0, concat_axis=0, tiled=True)  4.94 us
    all_to_all x1, starting transfers between devices, sent_to_all(): return lax.all_to_all(copies, axis, split_axis=0, concat_axis=0, tiled=True)  4.47 us
    reduce_sum x2, local copies, waits for them, and re-layouts, summed_on_arrival(): return arrived.sum(axis=0)  3.9 us
  transfers between devices with their start and end apart: 5, of which 4 were waited for; matrix products, arithmetic and copies ran while one was open for 11% of the time, Pallas kernels for 0%

commit v1 on v0

--- a/solution.py
+++ b/solution.py
@@ -4,52 +4,39 @@
 from jax.sharding import Mesh
 from jax.sharding import PartitionSpec as P
 
-SLIDE = ("slide_0", "slide_1", "slide_2")
-SLIDE_REP = ("slide_0", "slide_1", "slide_2", "rep")
-
-
-def split_up(shard, dim, size):
-    lengths = shard.shape
-    pieces = shard.reshape(*lengths[:dim], size, lengths[dim] // size, *lengths[dim + 1 :])
-    return jnp.moveaxis(pieces, dim, 0)
-
-
-def summed_on_arrival(shard, axis, dim):
-    pieces = split_up(shard, dim, lax.axis_size(axis))
-    arrived = lax.all_to_all(pieces, axis, split_axis=0, concat_axis=0, tiled=True)
-    return arrived.sum(axis=0)
-
-
-def sum_in_two_steps(shard, axes, dim):
-    far, near = axes
-    pieces = split_up(shard, dim, lax.axis_size(far))
-    nearer = summed_on_arrival(pieces, near, dim + 1)
-    arrived = lax.all_to_all(nearer, far, split_axis=0, concat_axis=0, tiled=True)
-    return arrived.sum(axis=0)
-
-
-def in_one_piece(arrays, axis, dim, along):
-    widths = [a.shape[along] for a in arrays]
-    both = jnp.concatenate(arrays, axis=along)
-    whole = sum_in_two_steps(both, axis, dim)
-    return tuple(jnp.split(whole, [sum(widths[:k]) for k in range(1, len(widths))], axis=along))
-
-
-def sent_to_all(shard, axis):
-    copies = jnp.broadcast_to(shard, (lax.axis_size(axis), *shard.shape))
-    return lax.all_to_all(copies, axis, split_axis=0, concat_axis=0, tiled=True)
-
-
-def over_copies(shard, axis):
-    return sent_to_all(shard, axis).sum(axis=0)
-
-
-def together(arrays, axis):
-    ends = [0]
-    for a in arrays:
-        ends.append(ends[-1] + a.size)
-    total = over_copies(jnp.concatenate([a.ravel() for a in arrays]), axis)
-    return tuple((total[b:e].reshape(a.shape) for a, b, e in zip(arrays, ends, ends[1:])))
+SLIDE = ("x", "z_high", "z_low", "core")
+SLIDE_REP = ("x", "z_high", "z_low", "core", "rep")
+
+
+def exchange(pieces, axis):
+    return lax.all_to_all(pieces, axis, split_axis=0, concat_axis=0, tiled=True)
+
+
+def summed(pieces, axis):
+    return exchange(pieces, axis).astype(jnp.float32).sum(axis=0)
+
+
+def scatter_sum(stacked):
+    width = stacked.shape[-1]
+    part = summed(stacked, "core").astype(jnp.bfloat16)
+    part = summed(part.reshape(4, part.shape[0] // 4, width), "x").astype(jnp.bfloat16)
+    part = summed(part.reshape(4, part.shape[0] // 4, width), "z_low").astype(jnp.bfloat16)
+    part = summed(part.reshape(4, part.shape[0] // 4, width), "z_high")
+    return summed(jnp.broadcast_to(part, (4, *part.shape)), "rep")
+
+
+def regrouping(hidden):
+    share = hidden // 128
+    row = jnp.arange(hidden, dtype=jnp.int32)
+    slot, slide = row % share, row // share
+    core, z, x = slide % 2, slide // 2 % 16, slide // 32
+    order = ((core * 4 + x) * 4 + z % 4) * 4 + z // 4
+    target = order * share + slot
+    return (target[:, None] == row[None, :]).astype(jnp.bfloat16)
+
+
+def regrouped(values, placing):
+    return jnp.dot(values, placing, preferred_element_type=jnp.float32).astype(jnp.bfloat16)
 
 
 def depthwise(field, kernel):
@@ -88,6 +75,11 @@
         inward_two,
         outward_two,
     ) = weights
+    placing = regrouping(inward_one.shape[1])
+    inward_one = regrouped(inward_one, placing)
+    outward_one = jnp.dot(placing.T, outward_one, preferred_element_type=jnp.float32).astype(
+        jnp.bfloat16
+    )
     slot_count = tile_feats.shape[0]
     side_cells = tile_feats.shape[1]
     narrow_width = tile_feats.shape[3]
@@ -142,7 +134,9 @@
     back_merged = (
         flat_cot.astype(jnp.float32) + back_depth.reshape(second_rows, wide_width)
     ).astype(jnp.bfloat16)
-    grad_project = jnp.dot(patches.T, back_merged, preferred_element_type=jnp.float32)
+    grad_project = jnp.dot(
+        regrouped(patches, placing).T, back_merged, preferred_element_type=jnp.float32
+    )
     back_patches = jnp.dot(back_merged, project_down.T, preferred_element_type=jnp.float32).astype(
         jnp.bfloat16
     )
@@ -161,7 +155,7 @@
     )
     unused, gelu_back = jax.vjp(gelu_exact, expand)
     back_expand = gelu_back(back_hidden.astype(jnp.float32))[0].astype(jnp.bfloat16)
-    grad_inward = jnp.dot(normed.T, back_expand, preferred_element_type=jnp.float32)
+    grad_inward = jnp.dot(back_expand.T, normed, preferred_element_type=jnp.float32)
     return (
         features.reshape(slot_count, half_side, half_side, wide_width),
         grad_inward,
@@ -203,35 +197,24 @@
         outward_two,
     )
     candidates = tile_feats.shape[0]
-    ordering = keep_list[0]
-    kept_count = tile_plan[0, 0]
     positions = jnp.arange(candidates, dtype=jnp.int32)
-    live = positions < kept_count
+    kept = jnp.logical_and(
+        keep_list[0][None, :] == positions[:, None], positions[None, :] < tile_plan[0, 0]
+    ).any(axis=1)
     zero_value = jnp.zeros((), jnp.bfloat16)
-    ordered_tiles = jnp.where(column_mask(live, 3), tile_feats[ordering], zero_value)
-    ordered_cot = jnp.where(column_mask(live, 3), cotangent[ordering], zero_value)
-    position_feats, grad_inward, grad_outward, grad_project = slot_pass(
-        ordered_tiles, ordered_cot, weights
-    )
-    place = jnp.sum(
-        jnp.where(ordering[None, :] == positions[:, None], positions[None, :], 0), axis=1
-    )
-    features = jnp.where(column_mask(place < kept_count, 3), position_feats[place], zero_value)
-    shares = (
-        sum_in_two_steps(grad_inward, (("slide_0", "slide_1"), "slide_2"), 1),
-        *in_one_piece((grad_outward, grad_project), (("slide_0", "slide_1"), "slide_2"), 0, 1),
-    )
-    summed = together((shares[0], shares[1], shares[2]), "rep")
-    inward_share = summed[0]
-    outward_share = summed[1]
-    project_share = summed[2]
-    return (features, inward_share, outward_share, project_share)
+    own_tiles = jnp.where(column_mask(kept, 3), tile_feats, zero_value)
+    own_cot = jnp.where(column_mask(kept, 3), cotangent, zero_value)
+    tile_features, grad_inward, grad_outward, grad_project = slot_pass(own_tiles, own_cot, weights)
+    features = jnp.where(column_mask(kept, 3), tile_features, zero_value)
+    stacked = jnp.concatenate([grad_inward, grad_outward, grad_project], axis=1)
+    rows, width = stacked.shape
+    share = scatter_sum(stacked.astype(jnp.bfloat16).reshape(2, rows // 2, width))
+    narrow = grad_inward.shape[1]
+    return (features, share[:, :narrow].T, share[:, narrow : 2 * narrow], share[:, 2 * narrow :])
 
 
 def solution(mesh):
-    split = Mesh(
-        mesh.devices.reshape(4, 16, 2, mesh.shape["rep"]), ("slide_0", "slide_1", "slide_2", "rep")
-    )
+    split = Mesh(mesh.devices.reshape(4, 4, 4, 2, mesh.shape["rep"]), SLIDE_REP)
     return jax.shard_map(
         per_device,
         mesh=split,

time: 183 us -> 99.8 us (0.55)
  waiting for transfers between devices: 93.6 us -> 5.16 us
  blocking collectives: 0 us -> 55.1 us
  starting transfers between devices: 38.6 us -> 4.47 us
  local copies, waits for them, and re-layouts: 20.7 us -> 7.74 us
  other arithmetic: 11.1 us -> 7.11 us
    all_to_all x5 -> x1, waiting for transfers between devices: 93.6 us -> 5.16 us  [exchange(): return lax.all_to_all(pieces, axis, split_axis=0, concat_axis=0, tiled=True)]
    all_to_all x0 -> x4, blocking collectives: none -> 55.1 us  [exchange(): return lax.all_to_all(pieces, axis, split_axis=0, concat_axis=0, tiled=True)]
    all_to_all x5 -> x1, starting transfers between devices: 38.6 us -> 4.47 us  [exchange(): return lax.all_to_all(pieces, axis, split_axis=0, concat_axis=0, tiled=True)]
    reduce_sum x6 -> x5, other arithmetic: 4.53 us -> 0.7 us  [summed(): return exchange(pieces, axis).astype(jnp.float32).sum(axis=0)]
    reduce_sum x3 -> x1, local copies, waits for them, and re-layouts: 4.02 us -> 0.26 us  [summed(): return exchange(pieces, axis).astype(jnp.float32).sum(axis=0)]
    transpose x1 -> x0, local copies, waits for them, and re-layouts: 3.63 us -> none  [split_up(): return jnp.moveaxis(pieces, dim, 0)]
    gather x5 -> x0, local copies, waits for them, and re-layouts: 3.58 us -> none  [the longest x2 1.56 us: per_device(): tile_feats[ordering]]
  transfers between devices with their start and end apart: 5 -> 1, of which waited for: 4 -> 1; matrix products, arithmetic and copies ran while one was open for 11% -> 1% of each run, Pallas kernels for 0% -> 0%
where the time goes in v1:
time: 99.8 us; the launch traced here: 98.5 us
  blocking collectives  55.1 us (55%)
  matrix products  17.7 us (18%)
  local copies, waits for them, and re-layouts  7.74 us (8%)
  other arithmetic  7.11 us (7%)
  waiting for transfers between devices  5.16 us (5%)
  starting transfers between devices  4.47 us (4%)
  between operations  1.15 us (1%)
    all_to_all x4, blocking collectives, exchange(): return lax.all_to_all(pieces, axis, split_axis=0, concat_axis=0, tiled=True)  55.1 us
    all_to_all x1, waiting for transfers between devices, exchange(): return lax.all_to_all(pieces, axis, split_axis=0, concat_axis=0, tiled=True)  5.16 us
    all_to_all x1, starting transfers between devices, exchange(): return lax.all_to_all(pieces, axis, split_axis=0, concat_axis=0, tiled=True)  4.47 us
    conv_general_dilated x3, matrix products, depthwise(): lax.conv_general_dilated(field.astype(jnp.float32), kernel.astype(jnp.flo...  4.21 us
    dot_general x1, matrix products, slot_pass(): jnp.dot(back_expand_two, inward_two.T, preferred_element_type=jnp.float32)  3.23 us
    dot_general x1, matrix products, slot_pass(): expand = jnp.dot(normed, inward_one, preferred_element_type=jnp.float32)  3.21 us
    unnamed x35, local copies, waits for them, and re-layouts  3.12 us
    dot_general x1, matrix products, slot_pass(): jnp.dot(back_section, outward_one.T, preferred_element_type=jnp.float32)  2.14 us
  transfers between devices with their start and end apart: 1, of which 1 were waited for; matrix products, arithmetic and copies ran while one was open for 1% of the time, Pallas kernels for 0%

profile of v1, /device:TPU:6, one launch (start us, length us, event | category | flops | bytes accessed | tf_op | source)
XLA Modules:
  0.0 98.5 jit_solution(1265457221681317423)
XLA Ops:
  0.7 0.7 iota_compare_fusion.13
  1.4 0.7 convert_element_type.142
  2.1 0.7 convert_element_type.135
  2.8 0.7 convert_element_type.146
  3.4 0.8 fusion.99
  4.2 1.0 %broadcast_select_fusion = bf16[4,8,8,192]{3,2,1,0:T(8,128)(2,1)S(1)} fusion(bf16[4,8,8,192]{3,2,1,0:T(8,128)(2,1)} %param.14, pred[4]{0:T(512)(128)(4,1)S(1)} %fusion.99), kind=kLoop, calls=%fused_computation.111 | loop fusion | flops 49152 | bytes 196612 | tf_op jit(solution)/shard_map/jit(_where)/select_n | solution.py:205
  5.4 2.2 %fusion.110 = (f32[4,8,8]{0,2,1:T(8,128)S(1)}, f32[4,8,8,192]{3,0,2,1:T(4,128)S(1)}) fusion(bf16[7,7,1,192]{3,1,0,2:T(8,128)(2,1)} %bitcast.126, bf16[4,8,8,192]{3,2,1,0:T(8,128)(2,1)S(1)} %broadcast_select_fusion), kind=kOutput, calls=%fused_computation.202 | convolution fusion | flops 3022592 | bytes 314752 | tf_op jit(solution)/shard_map/conv_general_dilated | solution.py:43
  7.6 0.3 multiply_reduce_fusion
  7.9 0.2 multiply_convert_fusion.1
  8.2 0.7 fusion.6
  8.8 3.2 %fusion.19 = (bf16[256,768]{1,0:T(8,128)(2,1)S(1)}, f32[256,768]{1,0:T(8,128)}) fusion(bf16[256,192]{1,0:T(8,128)(2,1)S(1)} %bitcast.120, bf16[192,768]{1,0:T(8,128)(2,1)S(1)} %copy-done.14, s32[768]{0:T(1024)S(1)} %fusion.86), kind=kOutput, calls=%fused_computation.33 | convolution fusion | flops 315506688 | bytes 1575936 | tf_op jit(solution)/shard_map/dot_general | solution.py:95
  12.0 0.3 fusion.111
  12.6 0.4 copy-done.8
  13.3 0.1 reshape.236
  13.5 1.2 %fusion.13 = bf16[768,64]{0,1:T(8,128)(2,1)} fusion(bf16[64,768]{1,0:T(8,128)(2,1)S(1)} %reshape.236, s32[768]{0:T(1024)S(1)} %fusion.86), kind=kOutput, calls=%fused_computation.23 | convolution fusion | flops 76136448 | bytes 199680 | tf_op jit(solution)/shard_map/dot_general | solution.py:39
  14.7 0.2 convolution_convert_fusion.7
  14.9 0.6 fusion.112
  15.6 0.2 multiply_reduce_fusion.4
  16.0 0.3 fusion.113
  16.3 0.9 copy-done.12
  17.2 1.0 %fusion.15 = bf16[64,384]{1,0:T(8,128)(2,1)S(1)} fusion(bf16[1536,384]{1,0:T(8,128)(2,1)S(1)} %copy-done.12, f32[64,1536]{1,0:T(8,128)S(1)} %fusion.113, bf16[64,384]{1,0:T(8,128)(2,1)S(1)} %convolution_convert_fusion.7), kind=kOutput, calls=%fused_computation.27 | convolution fusion | flops 81960960 | bytes 1671168 | tf_op jit(solution)/shard_map/dot_general | solution.py:119
  18.4 3.2 %fusion.16 = f32[64,384]{1,0:T(8,128)} fusion(bf16[384,1536]{1,0:T(8,128)(2,1)S(1)} %copy-done, bf16[64,384]{1,0:T(8,128)(2,1)S(1)} %reshape.240, bf16[1536,384]{1,0:T(8,128)(2,1)} %param.27, f32[64,1536]{1,0:T(8,128)S(1)} %fusion.113), kind=kOutput, calls=%fused_computation.29 | convolution fusion | flops 158318592 | bytes 2899968 | tf_op jit(solution)/shard_map/dot_general | solution.py:127
  21.7 0.9 reshape.249
  22.6 0.2 multiply_reduce_fusion.3
  22.8 0.2 fusion.105
  23.0 1.4 %add_convert_fusion.2 = (bf16[4,4,4,384]{3,0,2,1:T(4,128)(2,1)S(1)}, f32[4,4,4,384]{3,0,2,1:T(4,128)S(1)}) fusion(bf16[4,4,4,384]{3,0,2,1:T(4,128)(2,1)S(1)} %get-tuple-element.32, bf16[7,7,384,1]{2,1,0,3:T(8,128)(2,1)} %bitcast.124, f32[4,4,4]{0,2,1:T(4,128)S(1)} %negate_multiply_fusion.3, f32[4,4,4]{0,2,1:T(4,128)S(1)} %multiply_multiply_fusion.10, ...), kind=kOutput, calls=%fused_computation.116 | convolution fusion | flops 4964352 | bytes 433408 | tf_op jit(solution)/shard_map/transpose(jvp())/conv_general_dilated | solution.py:43
  24.5 0.3 fusion.14
  24.9 0.2 reshape.251
  25.2 0.2 reshape.250
  25.8 0.2 convolution_convert_fusion.3
  26.0 0.6 copy-done.16
  26.7 2.1 %fusion.24 = bf16[768,256]{0,1:T(8,128)(2,1)S(1)} fusion(bf16[768,192]{0,1:T(8,128)(2,1)S(1)} %fusion.6, f32[256,768]{1,0:T(8,128)S(1)} %copy-done.16, f32[256,192]{0,1:T(8,128)S(1)} %get-tuple-element.29, f32[256]{0:T(256)S(1)} %negate_multiply_fusion.4), kind=kOutput, calls=%fused_computation.38 | convolution fusion | flops 90144768 | bytes 1672192 | tf_op jit(solution)/shard_map/dot_general | solution.py:153
  28.8 0.2 copy.158
  29.0 0.3 convolution_convert_fusion.4
  29.3 0.4 copy-done.2
  29.7 0.4 convolution_convert_fusion.1
  30.2 4.7 %all_to_all.25 = bf16[2,384,768]{1,2,0:T(8,128)(2,1)S(1)} all-to-all(bf16[2,384,768]{1,2,0:T(8,128)(2,1)S(1)} %pad_maximum_fusion), channel_id=1, replica_groups=mesh['x'=4,'z_high'=4,'z_low'=4,'core'=2,'rep'=4] {'core'}, dimensions={0} | all-to-all | bytes 2359296 | tf_op jit(solution)/shard_map/all_to_all | solution.py:12
  34.9 0.6 reduce_sum.186
  35.4 0.3 copy.153
  35.7 16.9 %all_to_all.26 = bf16[4,96,768]{2,1,0:T(8,128)(2,1)S(1)} all-to-all(bf16[4,96,768]{2,1,0:T(8,128)(2,1)S(1)} %bitcast.114), channel_id=1, replica_groups=mesh['x'=4,'z_high'=4,'z_low'=4,'core'=2,'rep'=4] {'x'}, dimensions={0} | all-to-all | bytes 1179648 | tf_op jit(solution)/shard_map/all_to_all | solution.py:12
  52.7 9.0 %all_to_all.27 = bf16[4,24,768]{2,1,0:T(8,128)(2,1)S(1)} all-to-all(bf16[4,24,768]{2,1,0:T(8,128)(2,1)S(1)} %bitcast.119), channel_id=1, replica_groups=mesh['x'=4,'z_high'=4,'z_low'=4,'core'=2,'rep'=4] {'z_low'}, dimensions={0} | all-to-all | bytes 294912 | tf_op jit(solution)/shard_map/all_to_all | solution.py:12
  61.8 24.5 %all_to_all.28 = bf16[4,6,768]{2,1,0:T(8,128)(2,1)S(1)} all-to-all(bf16[4,6,768]{2,1,0:T(8,128)(2,1)S(1)} %reshape.246), channel_id=1, replica_groups=mesh['x'=4,'z_high'=4,'z_low'=4,'core'=2,'rep'=4] {'z_high'}, dimensions={0} | all-to-all | bytes 73728 | tf_op jit(solution)/shard_map/all_to_all | solution.py:12
  86.3 0.6 broadcast_in_dim.83
  86.9 4.5 %all-to-all-start.4 = ((f32[4,6,768]{2,1,0:T(8,128)}), f32[4,6,768]{2,1,0:T(8,128)S(1)}, u32[]{:S(2)}, u32[]{:S(2)}) async-start(f32[4,6,768]{2,1,0:T(8,128)} %broadcast_in_dim.83), calls=%async_computation.4 | async-start | bytes 196608 | tf_op jit(solution)/shard_map/all_to_all | solution.py:12
  91.4 0.6 copy.155
  92.0 5.2 %all-to-all-done.4 = f32[4,6,768]{2,1,0:T(8,128)S(1)} async-done(((f32[4,6,768]{2,1,0:T(8,128)}), f32[4,6,768]{2,1,0:T(8,128)S(1)}, u32[]{:S(2)}, u32[]{:S(2)}) %all-to-all-start.4) | async-done | bytes 73760 | tf_op jit(solution)/shard_map/all_to_all | solution.py:12
  97.2 0.6 slice.18
  97.8 0.7 fusion.109
  (72 shorter events, 2.0 us)
Async XLA Ops:
  0.6 15.3 %copy-start = (bf16[384,1536]{1,0:T(8,128)(2,1)S(1)}, bf16[384,1536]{1,0:T(8,128)(2,1)}, u32[]{:S(2)}) copy-start(bf16[384,1536]{1,0:T(8,128)(2,1)} %param.26) | copy-start | bytes 3538948
  2.1 10.4 %copy-start.4 = (f32[192]{0:T(256)}, f32[192]{0:T(256)S(1)}, u32[]{:S(2)}) copy-start(f32[192]{0:T(256)S(1)} %convert_element_type.142) | copy-start | bytes 2308
  4.2 3.9 %copy-start.10 = (pred[4]{0:T(512)(128)(4,1)}, pred[4]{0:T(512)(128)(4,1)S(1)}, u32[]{:S(2)}) copy-start(pred[4]{0:T(512)(128)(4,1)S(1)} %fusion.99) | copy-start | bytes 16
  5.2 2.9 %copy-start.13 = (bf16[768,192]{0,1:T(8,128)(2,1)S(1)}, bf16[768,192]{0,1:T(8,128)(2,1)}, u32[]{:S(2)}) copy-start(bf16[768,192]{0,1:T(8,128)(2,1)} %param.21) | copy-start | bytes 884740
  7.9 1.0 copy-start.14
  12.4 2.3 %copy-start.1 = (bf16[768,384]{1,0:T(8,128)(2,1)S(1)}, bf16[768,384]{1,0:T(8,128)(2,1)}, u32[]{:S(2)}) copy-start(bf16[768,384]{1,0:T(8,128)(2,1)} %param.23) | copy-start | bytes 1769476
  12.4 0.6 copy-start.8
  12.5 0.6 copy-start.6
  13.1 1.8 %copy-start.15 = (bf16[7,7,384]{2,1,0:T(8,128)(2,1)S(1)}, bf16[7,7,384]{2,1,0:T(8,128)(2,1)}, u32[]{:S(2)}) copy-start(bf16[7,7,384]{2,1,0:T(8,128)(2,1)} %param.24) | copy-start | bytes 112900
  16.0 1.3 %copy-start.12 = (bf16[1536,384]{1,0:T(8,128)(2,1)S(1)}, bf16[1536,384]{1,0:T(8,128)(2,1)}, u32[]{:S(2)}) copy-start(bf16[1536,384]{1,0:T(8,128)(2,1)} %param.27) | copy-start | bytes 3538948
  17.2 1.0 %copy-start.3 = (bf16[4,4,4,384]{3,2,1,0:T(4,128)(2,1)S(1)}, bf16[4,4,4,384]{3,2,1,0:T(4,128)(2,1)}, u32[]{:S(2)}) copy-start(bf16[4,4,4,384]{3,2,1,0:T(4,128)(2,1)} %param.15) | copy-start | bytes 147460
  17.2 1.0 %copy-start.11 = (pred[4]{0:T(512)(128)(4,1)S(1)}, pred[4]{0:T(512)(128)(4,1)}, u32[]{:S(2)}) copy-start(pred[4]{0:T(512)(128)(4,1)} %copy-done.10) | copy-start | bytes 16
  24.8 0.7 copy-start.5
  24.8 0.8 copy-start.9
  24.9 0.8 copy-start.7
  25.5 1.1 %copy-start.16 = (f32[256,768]{1,0:T(8,128)S(1)}, f32[256,768]{1,0:T(8,128)}, u32[]{:S(2)}) copy-start(f32[256,768]{1,0:T(8,128)} %get-tuple-element.37) | copy-start | bytes 2359300
  28.8 0.9 copy-start.2
  86.9 10.3 %all-to-all-start.4 = ((f32[4,6,768]{2,1,0:T(8,128)}), f32[4,6,768]{2,1,0:T(8,128)S(1)}, u32[]{:S(2)}, u32[]{:S(2)}) async-start(f32[4,6,768]{2,1,0:T(8,128)} %broadcast_in_dim.83), calls=%async_computation.4 | async-start | bytes 196608 | tf_op jit(solution)/shard_map/all_to_all | solution.py:12

commit v2 on v1

v2 whole, which is shorter than its diff:
```python
import jax
import jax.numpy as jnp
from jax import lax
from jax.experimental import pallas as pl
from jax.experimental.pallas import tpu as pltpu
from jax.sharding import Mesh
from jax.sharding import PartitionSpec as P

SLIDE = ("x", "z", "core")
SLIDE_REP = ("x", "z", "core", "rep")
F32 = jnp.float32
BF16 = jnp.bfloat16
TILES = 4
CELLS = 16
NARROW = 192
WIDE = 384
HIDDEN = 768
HIDDEN_TWO = 1536
ROWS = 256
ROWS_TWO = 64
HALF_ROOT = 0.7071067811865476
DENSITY = 0.3989422804014327


def product(left, right, contract=(1, 0)):
    return lax.dot_general(
        left, right, (((contract[0],), (contract[1],)), ((), ())), preferred_element_type=F32
    )


def statistics(values, eps=1e-6):
    offset = values - jnp.mean(values, axis=-1, keepdims=True)
    scale = lax.rsqrt(jnp.mean(offset * offset, axis=-1, keepdims=True) + eps)
    return offset * scale, scale


def norm_back(scaled, scale, gained):
    mean = jnp.mean(gained, axis=-1, keepdims=True)
    along = jnp.mean(gained * scaled, axis=-1, keepdims=True)
    return scale * (gained - mean - scaled * along)


def gelu_parts(values):
    below = 0.5 + 0.5 * lax.erf(values * HALF_ROOT)
    return values * below, below + values * (DENSITY * jnp.exp(-0.5 * values * values))


def gelu_rows(expand_ref, hidden_ref, block):
    def step(index, carry):
        rows = pl.ds(pl.multiple_of(index * block, block), block)
        hidden, slope = gelu_parts(expand_ref[rows, :])
        hidden_ref[rows, :] = hidden.astype(BF16)
        expand_ref[rows, :] = slope
        return carry

    lax.fori_loop(0, expand_ref.shape[0] // block, step, 0)


def slope_rows(slope_ref, back_ref, block):
    def step(index, carry):
        rows = pl.ds(pl.multiple_of(index * block, block), block)
        back_ref[rows, :] = (slope_ref[rows, :] * back_ref[rows, :].astype(F32)).astype(BF16)
        return carry

    lax.fori_loop(0, slope_ref.shape[0] // block, step, 0)


def one_hot(shape, source, source_dim):
    own = lax.broadcasted_iota(jnp.int32, shape, 1 - source_dim)
    index = lax.broadcasted_iota(jnp.int32, shape, source_dim)
    return jnp.where(own == source(index), 1.0, 0.0).astype(BF16)


def hidden_source(place):
    third, rest = place >> 8, place & 255
    core, pair, low = rest >> 7, (rest >> 1) & 63, rest & 1
    return (pair * 2 + core) * 6 + third * 2 + low


def row_source(place):
    tile, x, y = place & 3, (place >> 2) & 3, (place >> 4) & 3
    column, row = (place >> 6) & 1, place >> 7
    return tile * 64 + (2 * y + row) * 8 + 2 * x + column


def cell_source(place):
    return (place & 3) * 16 + (place >> 2)


def tile_place(place):
    return (place & 15) * 4 + (place >> 4)


def conv_one(tile, kernel_ref):
    cell = lax.broadcasted_iota(jnp.int32, (8, NARROW), 0)
    sums = [None] * 8
    for dx in range(-3, 4):
        inside = jnp.logical_and(cell + dx >= 0, cell + dx < 8)
        taps = [jnp.broadcast_to(kernel_ref[dy, dx + 3 : dx + 4, :], (8, NARROW)) for dy in range(7)]
        for source in range(8):
            line = tile[source]
            if dx != 0:
                line = jnp.where(inside, pltpu.roll(line, (-dx) % 8, 0), 0.0)
            for target in range(max(0, source - 3), min(8, source + 4)):
                term = taps[source - target + 3] * line
                sums[target] = term if sums[target] is None else sums[target] + term
    return jnp.concatenate(sums, axis=0)


def conv_two(source_ref, kernel_ref, out_ref, back):
    for part in range(WIDE // 128):
        lanes = slice(part * 128, part * 128 + 128)
        cells = [source_ref[4 * c : 4 * c + 8, lanes] for c in range(CELLS)]
        taps = {}
        for dy in range(7):
            for dx in range(7):
                taps[dy, dx] = jnp.broadcast_to(kernel_ref[dy, dx : dx + 1, lanes], (8, 128))
        for y in range(4):
            for x in range(4):
                total = None
                for fy in range(4):
                    for fx in range(4):
                        dy, dx = (y - fy, x - fx) if back else (fy - y, fx - x)
                        term = taps[dy + 3, dx + 3] * cells[fy * 4 + fx]
                        total = term if total is None else total + term
                place = 4 * (y * 4 + x)
                out_ref[place : place + 4, lanes] = total[0:4]


def step_kernel(
    keep_ref,
    plan_ref,
    feats_ref,
    cot_ref,
    kernel_one_ref,
    gain_one_ref,
    inward_one_ref,
    outward_one_ref,
    gain_down_ref,
    project_ref,
    kernel_two_ref,
    gain_two_ref,
    inward_two_ref,
    outward_two_ref,
    features_ref,
    grads_ref,
    taps_one,
    taps_two,
    field,
    normed_rows,
    expand,
    hidden,
    back_hidden,
    expand_two,
    hidden_two,
    back_two,
    padded,
    spread,
):
    count = plan_ref[0, 0]
    kept = []
    for tile in range(TILES):
        place = jnp.int32(0)
        for position in range(TILES):
            place = place + jnp.where(keep_ref[0, position] == tile, position, 0)
        kept.append(place < count)
    taps_one[...] = kernel_one_ref[...].astype(F32)
    taps_two[...] = kernel_two_ref[...].astype(F32)
    gain_one = gain_one_ref[...].astype(F32)
    gain_down = gain_down_ref[...].astype(F32)
    gain_two = gain_two_ref[...].astype(F32)

    placing = one_hot((HIDDEN, HIDDEN), hidden_source, 1)
    inward = product(inward_one_ref[...], placing).astype(BF16)
    outward = product(outward_one_ref[...], placing).astype(BF16)

    for tile in range(TILES):
        own = jnp.where(kept[tile], feats_ref[tile].astype(F32), 0.0)
        rows = slice(tile * 64, tile * 64 + 64)
        field[rows, :] = own.reshape(64, NARROW).astype(BF16)
        scaled, _ = statistics(conv_one(own, taps_one))
        normed_rows[rows, :] = (scaled * gain_one).astype(BF16)

    gather_rows = one_hot((ROWS, ROWS), row_source, 0)
    normed = product(gather_rows, normed_rows[...]).astype(BF16)
    field_rows = product(gather_rows, field[...])
    expand[...] = product(normed, inward)
    gelu_rows(expand, hidden, 16)
    section = (field_rows + product(hidden[...], outward, (1, 1))).astype(BF16).astype(F32)
    scaled_down, scale_down = statistics(section)
    down = (scaled_down * gain_down).astype(BF16)
    merged = None
    for block in range(4):
        part = product(
            down[block * 64 : block * 64 + 64], project_ref[block * NARROW : (block + 1) * NARROW, :]
        )
        merged = part if merged is None else merged + part
    merged = merged.astype(BF16).astype(F32)

    padded[0:ROWS_TWO, :] = merged
    padded[ROWS_TWO : ROWS_TWO + 8, :] = jnp.zeros((8, WIDE), F32)
    conv_two(padded, taps_two, spread, False)
    scaled_two, scale_two = statistics(spread[...])
    normed_two = (scaled_two * gain_two).astype(BF16)
    expand_two[...] = product(normed_two, inward_two_ref[...])
    gelu_rows(expand_two, hidden_two, 16)
    features = (merged + product(hidden_two[...], outward_two_ref[...])).astype(BF16)
    scatter_cells = one_hot((ROWS_TWO, ROWS_TWO), tile_place, 0)
    spread[...] = product(scatter_cells, features)
    for index in range(CELLS):
        tile, y = index // 4, index % 4
        own = spread[4 * index : 4 * index + 4, :]
        features_ref[tile, y] = jnp.where(kept[tile], own, 0.0).astype(BF16)

    for index in range(CELLS):
        tile, y = index // 4, index % 4
        own = jnp.where(kept[tile], cot_ref[tile, y].astype(F32), 0.0)
        spread[4 * index : 4 * index + 4, :] = own
    gather_cells = one_hot((ROWS_TWO, ROWS_TWO), cell_source, 0)
    flat_cot = product(gather_cells, spread[...].astype(BF16))
    back_two[...] = product(flat_cot.astype(BF16), outward_two_ref[...], (1, 1)).astype(BF16)
    slope_rows(expand_two, back_two, 16)
    back_normed_two = product(back_two[...], inward_two_ref[...], (1, 1)).astype(BF16).astype(F32)
    padded[0:ROWS_TWO, :] = norm_back(scaled_two, scale_two, back_normed_two * gain_two)
    conv_two(padded, taps_two, spread, True)
    back_merged = (flat_cot + spread[...]).astype(BF16)

    patches = None
    back_down = []
    for block in range(4):
        rows = slice(block * NARROW, (block + 1) * NARROW)
        part = product(down[block * 64 : block * 64 + 64], placing[rows, :])
        patches = part if patches is None else patches + part
        back_down.append(product(back_merged, project_ref[rows, :], (1, 1)))
    back_down = jnp.concatenate(back_down, axis=0).astype(BF16).astype(F32)
    grad_project = product(patches.astype(BF16), back_merged, (0, 0)).astype(BF16)
    back_section = norm_back(scaled_down, scale_down, back_down * gain_down).astype(BF16)
    back_hidden[...] = product(back_section, outward).astype(BF16)
    slope_rows(expand, back_hidden, 16)
    grad_outward = product(hidden[...], back_section, (0, 0)).astype(BF16)
    grad_inward = product(back_hidden[...], normed, (0, 0)).astype(BF16)
    for third in range(3):
        for core in range(2):
            rows = slice(third * 256 + core * 128, third * 256 + core * 128 + 128)
            left = third * HIDDEN
            grads_ref[core, :, left : left + NARROW] = grad_inward[rows]
            grads_ref[core, :, left + NARROW : left + WIDE] = grad_outward[rows]
            grads_ref[core, :, left + WIDE : left + HIDDEN] = grad_project[rows]


def local_step(*operands):
    smem = pl.BlockSpec(memory_space=pltpu.SMEM)
    vmem = pl.BlockSpec(memory_space=pltpu.VMEM)
    return pl.pallas_call(
        step_kernel,
        in_specs=[smem, smem] + [vmem] * 12,
        out_specs=[vmem, vmem],
        out_shape=[
            jax.ShapeDtypeStruct((TILES, 4, 4, WIDE), BF16),
            jax.ShapeDtypeStruct((2, 128, 3 * HIDDEN), BF16),
        ],
        scratch_shapes=[
            pltpu.VMEM((7, 7, NARROW), F32),
            pltpu.VMEM((7, 7, WIDE), F32),
            pltpu.VMEM((ROWS, NARROW), BF16),
            pltpu.VMEM((ROWS, NARROW), BF16),
            pltpu.VMEM((ROWS, HIDDEN), F32),
            pltpu.VMEM((ROWS, HIDDEN), BF16),
            pltpu.VMEM((ROWS, HIDDEN), BF16),
            pltpu.VMEM((ROWS_TWO, HIDDEN_TWO), F32),
            pltpu.VMEM((ROWS_TWO, HIDDEN_TWO), BF16),
            pltpu.VMEM((ROWS_TWO, HIDDEN_TWO), BF16),
            pltpu.VMEM((ROWS_TWO + 8, WIDE), F32),
            pltpu.VMEM((ROWS_TWO, WIDE), F32),
        ],
        name="local_step",
    )(*operands)


def pair_kernel(parts_ref, out_ref):
    def step(index, carry):
        rows = pl.ds(pl.multiple_of(index * 16, 16), 16)
        total = parts_ref[0, rows, :].astype(F32) + parts_ref[1, rows, :].astype(F32)
        for slide in range(8):
            out_ref[index * 8 + slide] = total[2 * slide : 2 * slide + 2].astype(BF16)
        return carry

    lax.fori_loop(0, parts_ref.shape[1] // 16, step, 0)


def pair_sum(parts):
    vmem = pl.BlockSpec(memory_space=pltpu.VMEM)
    return pl.pallas_call(
        pair_kernel,
        in_specs=[vmem],
        out_specs=vmem,
        out_shape=jax.ShapeDtypeStruct((64, 2, parts.shape[2]), BF16),
        name="pair_sum",
    )(parts)


def exchange(pieces, axis):
    return lax.all_to_all(pieces, axis, split_axis=0, concat_axis=0, tiled=True)


def per_device(
    tile_feats,
    cotangent,
    keep_list,
    tile_plan,
    kernel_one,
    gain_one,
    inward_one,
    outward_one,
    gain_down,
    project_down,
    kernel_two,
    gain_two,
    inward_two,
    outward_two,
):
    features, grads = local_step(
        keep_list,
        tile_plan,
        tile_feats,
        cotangent,
        kernel_one,
        gain_one.reshape(1, NARROW),
        inward_one,
        outward_one.T,
        gain_down.reshape(1, NARROW),
        project_down,
        kernel_two,
        gain_two.reshape(1, WIDE),
        inward_two,
        outward_two,
    )
    own = pair_sum(exchange(grads, "core"))
    own = exchange(own, ("x", "z")).astype(F32).sum(axis=0)
    share = exchange(jnp.broadcast_to(own, (4, *own.shape)), "rep").sum(axis=0)
    share = share.reshape(2, 3, HIDDEN).transpose(1, 0, 2).reshape(6, HIDDEN)
    return (features, share[:, :NARROW].T, share[:, NARROW:WIDE], share[:, WIDE:])


def solution(mesh):
    split = Mesh(mesh.devices.reshape(4, 16, 2, mesh.shape["rep"]), SLIDE_REP)
    return jax.shard_map(
        per_device,
        mesh=split,
        in_specs=(
            P(SLIDE_REP, None, None, None),
            P(SLIDE_REP, None, None, None),
            P(SLIDE_REP, None),
            P(SLIDE_REP, None),
            P(),
            P(),
            P(),
            P(),
            P(),
            P(),
            P(),
            P(),
            P(),
            P(),
        ),
        out_specs=(P(SLIDE_REP, None, None, None), P(None, SLIDE), P(SLIDE, None), P(SLIDE, None)),
        check_vma=False,
    )
```

time: 99.8 us -> 90.6 us (0.908)
  matrix products: 17.7 us -> 0 us
  blocking collectives: 55.1 us -> 70.3 us
  Pallas kernels: 0 us -> 13.8 us
  other arithmetic: 7.11 us -> 0.53 us
  waiting for transfers between devices: 5.16 us -> 0 us
  starting transfers between devices: 4.47 us -> 0 us
  local copies, waits for them, and re-layouts: 7.74 us -> 5.03 us
    all_to_all x4 -> x3, blocking collectives: 55.1 us -> 70.3 us  [exchange(): return lax.all_to_all(pieces, axis, split_axis=0, concat_axis=0, tiled=True)]
    pallas_call x0 -> x2, Pallas kernels: none -> 13.8 us  [the longest x1 11.4 us: local_step(): pl.pallas_call(step_kernel, in_specs=[smem, smem] + [vmem] * 12, out_spec...]
    dot_general x13 -> x0, matrix products: 13.5 us -> none  [the longest x1 3.23 us: slot_pass(): jnp.dot(back_expand_two, inward_two.T, preferred_element_type=jnp.float32)]
    all_to_all x1 -> x0, waiting for transfers between devices: 5.16 us -> none  [exchange(): return lax.all_to_all(pieces, axis, split_axis=0, concat_axis=0, tiled=True)]
    all_to_all x1 -> x0, starting transfers between devices: 4.47 us -> none  [exchange(): return lax.all_to_all(pieces, axis, split_axis=0, concat_axis=0, tiled=True)]
    conv_general_dilated x3 -> x0, matrix products: 4.21 us -> none  [depthwise(): lax.conv_general_dilated(field.astype(jnp.float32), kernel.astype(jnp.flo...]
    unnamed x35 -> x0, local copies, waits for them, and re-layouts: 3.12 us -> none
    reshape x9 -> x5, local copies, waits for them, and re-layouts: 1.26 us -> 3.73 us  [the longest x1 1.24 us: per_device(): gain_two.reshape(1, WIDE)]
  transfers between devices with their start and end apart: 1 -> 0, of which waited for: 1 -> 0; matrix products, arithmetic and copies ran while one was open for 1% -> 0% of each run, Pallas kernels for 0% -> 0%
where the time goes in v2:
time: 90.6 us; the launch traced here: 90.2 us
  blocking collectives  70.3 us (78%)
  Pallas kernels  13.8 us (15%)
  local copies, waits for them, and re-layouts  5.03 us (6%)
    all_to_all x3, blocking collectives, exchange(): return lax.all_to_all(pieces, axis, split_axis=0, concat_axis=0, tiled=True)  70.3 us
    pallas_call x1, Pallas kernels, local_step(): pl.pallas_call(step_kernel, in_specs=[smem, smem] + [vmem] * 12, out_spec...  11.4 us
    pallas_call x1, Pallas kernels, pair_sum(): pl.pallas_call(pair_kernel, in_specs=[vmem], out_specs=vmem, out_shape=ja...  2.38 us

profile of v2, /device:TPU:6, one launch (start us, length us, event | category | flops | bytes accessed | tf_op | source)
XLA Modules:
  0.0 90.2 jit_solution(2750865651664210013)
XLA Ops:
  0.6 1.2 %reshape.23.gain_one_ref = bf16[1,192]{1,0:T(2,128)(2,1)} reshape(bf16[192]{0:T(256)(128)(2,1)} %param.19) | data formatting | bytes 768 | tf_op jit(solution)/shard_map/reshape | solution.py:328
  1.9 1.2 %reshape.24.gain_down_ref = bf16[1,192]{1,0:T(2,128)(2,1)} reshape(bf16[192]{0:T(256)(128)(2,1)} %param.22) | data formatting | bytes 768 | tf_op jit(solution)/shard_map/reshape | solution.py:331
  3.1 1.2 %reshape.25.gain_two_ref = bf16[1,384]{1,0:T(2,128)(2,1)} reshape(bf16[384]{0:T(512)(128)(2,1)} %param.25) | data formatting | bytes 1536 | tf_op jit(solution)/shard_map/reshape | solution.py:334
  4.3 11.4 %local_step.1 = (bf16[4,4,4,384]{3,2,1,0:T(4,128)(2,1)}, bf16[2,128,2304]{2,1,0:T(8,128)(2,1)}) custom-call(s32[1,4]{1,0:T(1,128)} %keep_ref.1, s32[1,2]{1,0:T(1,128)} %plan_ref.1, bf16[4,8,8,192]{3,2,1,0:T(8,128)(2,1)} %feats_ref.1, bf16[4,4,4,384]{3,2,1,0:T(4,128)(2,1)} %cot_ref.1, bf16[7,7,192]{2,1,0:T(8,128)(2,1)} %kernel_one_ref.1, ...), custom_call_target="tpu_custom_call" | custom-call | tf_op jit(solution)/shard_map/local_step/pallas_call | solution.py:254
  15.7 6.7 %all_to_all.15.parts_ref = bf16[2,128,2304]{2,1,0:T(8,128)(2,1)} all-to-all(bf16[2,128,2304]{2,1,0:T(8,128)(2,1)} %get-tuple-element.7), channel_id=1, replica_groups=mesh['x'=4,'z'=16,'core'=2,'rep'=4] {'core'}, dimensions={0} | all-to-all | bytes 2359296 | tf_op jit(solution)/shard_map/all_to_all | solution.py:303
  22.4 2.4 %pair_sum.1 = bf16[64,2,2304]{2,1,0:T(2,128)(2,1)} custom-call(bf16[2,128,2304]{2,1,0:T(8,128)(2,1)} %all_to_all.15.parts_ref), custom_call_target="tpu_custom_call" | custom-call | tf_op jit(solution)/shard_map/pair_sum/pallas_call | solution.py:293
  24.8 53.6 %all_to_all.16 = bf16[64,2,2304]{2,1,0:T(2,128)(2,1)S(1)} all-to-all(bf16[64,2,2304]{2,1,0:T(2,128)(2,1)} %pair_sum.1), channel_id=1, replica_groups=mesh['x'=4,'z'=16,'core'=2,'rep'=4] {'x','z'}, dimensions={0} | all-to-all | bytes 1179648 | tf_op jit(solution)/shard_map/all_to_all | solution.py:303
  78.4 0.5 convert_reduce_fusion
  78.9 9.9 %all_to_all.17 = f32[4,2,2304]{2,1,0:T(2,128)S(1)} all-to-all(f32[4,2,2304]{2,1,0:T(2,128)S(1)} %broadcast_in_dim.3), channel_id=1, replica_groups=mesh['x'=4,'z'=16,'core'=2,'rep'=4] {'rep'}, dimensions={0} | all-to-all | bytes 147456 | tf_op jit(solution)/shard_map/all_to_all | solution.py:303
  89.0 0.6 slice.14
  89.6 0.7 fusion
  (5 shorter events, 0.1 us)

commit v3 on v2

--- a/solution.py
+++ b/solution.py
@@ -166,9 +166,9 @@
         kept.append(place < count)
     taps_one[...] = kernel_one_ref[...].astype(F32)
     taps_two[...] = kernel_two_ref[...].astype(F32)
-    gain_one = gain_one_ref[...].astype(F32)
-    gain_down = gain_down_ref[...].astype(F32)
-    gain_two = gain_two_ref[...].astype(F32)
+    gain_one = gain_one_ref[...].astype(F32).reshape(1, NARROW)
+    gain_down = gain_down_ref[...].astype(F32).reshape(1, NARROW)
+    gain_two = gain_two_ref[...].astype(F32).reshape(1, WIDE)
 
     placing = one_hot((HIDDEN, HIDDEN), hidden_source, 1)
     inward = product(inward_one_ref[...], placing).astype(BF16)
@@ -277,10 +277,12 @@
     )(*operands)
 
 
-def pair_kernel(parts_ref, out_ref):
+def spread_kernel(parts_ref, out_ref):
     def step(index, carry):
         rows = pl.ds(pl.multiple_of(index * 16, 16), 16)
-        total = parts_ref[0, rows, :].astype(F32) + parts_ref[1, rows, :].astype(F32)
+        total = parts_ref[0, rows, :].astype(F32)
+        for part in range(1, parts_ref.shape[0]):
+            total = total + parts_ref[part, rows, :].astype(F32)
         for slide in range(8):
             out_ref[index * 8 + slide] = total[2 * slide : 2 * slide + 2].astype(BF16)
         return carry
@@ -288,14 +290,14 @@
     lax.fori_loop(0, parts_ref.shape[1] // 16, step, 0)
 
 
-def pair_sum(parts):
+def spread_sum(parts):
     vmem = pl.BlockSpec(memory_space=pltpu.VMEM)
     return pl.pallas_call(
-        pair_kernel,
+        spread_kernel,
         in_specs=[vmem],
         out_specs=vmem,
-        out_shape=jax.ShapeDtypeStruct((64, 2, parts.shape[2]), BF16),
-        name="pair_sum",
+        out_shape=jax.ShapeDtypeStruct((parts.shape[1] // 2, 2, parts.shape[2]), BF16),
+        name="spread_sum",
     )(parts)
 
 
@@ -325,18 +327,19 @@
         tile_feats,
         cotangent,
         kernel_one,
-        gain_one.reshape(1, NARROW),
+        gain_one,
         inward_one,
         outward_one.T,
-        gain_down.reshape(1, NARROW),
+        gain_down,
         project_down,
         kernel_two,
-        gain_two.reshape(1, WIDE),
+        gain_two,
         inward_two,
         outward_two,
     )
-    own = pair_sum(exchange(grads, "core"))
-    own = exchange(own, ("x", "z")).astype(F32).sum(axis=0)
+    own = exchange(grads, "core").astype(F32).sum(axis=0).astype(BF16)
+    own = spread_sum(exchange(own.reshape(4, 32, own.shape[1]), "x"))
+    own = exchange(own, "z").astype(F32).sum(axis=0)
     share = exchange(jnp.broadcast_to(own, (4, *own.shape)), "rep").sum(axis=0)
     share = share.reshape(2, 3, HIDDEN).transpose(1, 0, 2).reshape(6, HIDDEN)
     return (features, share[:, :NARROW].T, share[:, NARROW:WIDE], share[:, WIDE:])

time: 90.6 us -> 75.4 us (0.83); the launches traced: 90.2 us -> 74.1 us
  blocking collectives: 70.3 us -> 58.4 us
  local copies, waits for them, and re-layouts: 5.03 us -> 1.35 us
    all_to_all x3 -> x4, blocking collectives: 70.3 us -> 58.4 us  [exchange(): return lax.all_to_all(pieces, axis, split_axis=0, concat_axis=0, tiled=True)]
    reshape x3 -> x0, local copies, waits for them, and re-layouts: 3.68 us -> none  [the longest x1 1.24 us: per_device(): gain_two.reshape(1, WIDE)]
where the time goes in v3:
time: 75.4 us; the launch traced here: 74.1 us
  blocking collectives  58.4 us (77%)
  Pallas kernels  13.2 us (18%)
  local copies, waits for them, and re-layouts  1.35 us (2%)
    all_to_all x4, blocking collectives, exchange(): return lax.all_to_all(pieces, axis, split_axis=0, concat_axis=0, tiled=True)  58.4 us
    pallas_call x1, Pallas kernels, local_step(): pl.pallas_call(step_kernel, in_specs=[smem, smem] + [vmem] * 12, out_spec...  11.3 us
    pallas_call x1, Pallas kernels, spread_sum(): pl.pallas_call(spread_kernel, in_specs=[vmem], out_specs=vmem, out_shape=...  1.82 us

profile of v3, /device:TPU:6, one launch (start us, length us, event | category | flops | bytes accessed | tf_op | source)
XLA Modules:
  0.0 74.1 jit_solution(15200393626241869938)
XLA Ops:
  0.6 11.3 %local_step.1 = (bf16[4,4,4,384]{3,2,1,0:T(4,128)(2,1)}, bf16[2,128,2304]{2,1,0:T(8,128)(2,1)}) custom-call(s32[1,4]{1,0:T(1,128)} %keep_ref.1, s32[1,2]{1,0:T(1,128)} %plan_ref.1, bf16[4,8,8,192]{3,2,1,0:T(8,128)(2,1)} %feats_ref.1, bf16[4,4,4,384]{3,2,1,0:T(4,128)(2,1)} %cot_ref.1, bf16[7,7,192]{2,1,0:T(8,128)(2,1)} %kernel_one_ref.1, ...), custom_call_target="tpu_custom_call" | custom-call | tf_op jit(solution)/shard_map/local_step/pallas_call | solution.py:254
  12.0 5.8 %all_to_all.20 = bf16[2,128,2304]{2,1,0:T(8,128)(2,1)S(1)} all-to-all(bf16[2,128,2304]{2,1,0:T(8,128)(2,1)} %get-tuple-element.7), channel_id=1, replica_groups=mesh['x'=4,'z'=16,'core'=2,'rep'=4] {'core'}, dimensions={0} | all-to-all | bytes 2359296 | tf_op jit(solution)/shard_map/all_to_all | solution.py:305
  17.8 0.4 reduce_sum.30
  18.1 17.6 %all_to_all.21.parts_ref = bf16[4,32,2304]{2,1,0:T(8,128)(2,1)} all-to-all(bf16[4,32,2304]{2,1,0:T(8,128)(2,1)S(1)} %bitcast.5), channel_id=1, replica_groups=mesh['x'=4,'z'=16,'core'=2,'rep'=4] {'x'}, dimensions={0} | all-to-all | bytes 1179648 | tf_op jit(solution)/shard_map/all_to_all | solution.py:305
  35.7 1.8 %spread_sum.1 = bf16[16,2,2304]{2,1,0:T(2,128)(2,1)} custom-call(bf16[4,32,2304]{2,1,0:T(8,128)(2,1)} %all_to_all.21.parts_ref), custom_call_target="tpu_custom_call" | custom-call | tf_op jit(solution)/shard_map/spread_sum/pallas_call | solution.py:295
  37.6 25.1 %all_to_all.22 = bf16[16,2,2304]{2,1,0:T(2,128)(2,1)S(1)} all-to-all(bf16[16,2,2304]{2,1,0:T(2,128)(2,1)} %spread_sum.1), channel_id=1, replica_groups=mesh['x'=4,'z'=16,'core'=2,'rep'=4] {'z'}, dimensions={0} | all-to-all | bytes 294912 | tf_op jit(solution)/shard_map/all_to_all | solution.py:305
  62.7 0.1 convert_reduce_fusion
  62.8 9.9 %all_to_all.23 = f32[4,2,2304]{2,1,0:T(2,128)S(1)} all-to-all(f32[4,2,2304]{2,1,0:T(2,128)S(1)} %broadcast_in_dim.3), channel_id=1, replica_groups=mesh['x'=4,'z'=16,'core'=2,'rep'=4] {'rep'}, dimensions={0} | all-to-all | bytes 147456 | tf_op jit(solution)/shard_map/all_to_all | solution.py:305
  72.8 0.6 slice.14
  73.4 0.7 fusion
  (5 shorter events, 0.1 us)

commit v4 on v3

--- a/solution.py
+++ b/solution.py
@@ -1,5 +1,6 @@
 import jax
 import jax.numpy as jnp
+import numpy as np
 from jax import lax
 from jax.experimental import pallas as pl
 from jax.experimental.pallas import tpu as pltpu
@@ -45,24 +46,12 @@
     return values * below, below + values * (DENSITY * jnp.exp(-0.5 * values * values))
 
 
-def gelu_rows(expand_ref, hidden_ref, block):
-    def step(index, carry):
-        rows = pl.ds(pl.multiple_of(index * block, block), block)
-        hidden, slope = gelu_parts(expand_ref[rows, :])
-        hidden_ref[rows, :] = hidden.astype(BF16)
-        expand_ref[rows, :] = slope
-        return carry
-
-    lax.fori_loop(0, expand_ref.shape[0] // block, step, 0)
-
-
-def slope_rows(slope_ref, back_ref, block):
-    def step(index, carry):
-        rows = pl.ds(pl.multiple_of(index * block, block), block)
-        back_ref[rows, :] = (slope_ref[rows, :] * back_ref[rows, :].astype(F32)).astype(BF16)
-        return carry
-
-    lax.fori_loop(0, slope_ref.shape[0] // block, step, 0)
+def gelu_columns(rows, weights_ref, hidden_ref, slope_ref, block):
+    for left in range(0, slope_ref.shape[1], block):
+        columns = slice(left, left + block)
+        hidden, slope = gelu_parts(product(rows, weights_ref[:, columns]))
+        hidden_ref[:, columns] = hidden.astype(BF16)
+        slope_ref[:, columns] = slope
 
 
 def one_hot(shape, source, source_dim):
@@ -108,23 +97,34 @@
 
 
 def conv_two(source_ref, kernel_ref, out_ref, back):
+    low = lax.broadcasted_iota(jnp.int32, (8, 128), 0) < 4
     for part in range(WIDE // 128):
         lanes = slice(part * 128, part * 128 + 128)
-        cells = [source_ref[4 * c : 4 * c + 8, lanes] for c in range(CELLS)]
-        taps = {}
-        for dy in range(7):
-            for dx in range(7):
-                taps[dy, dx] = jnp.broadcast_to(kernel_ref[dy, dx : dx + 1, lanes], (8, 128))
+        cells = []
+        for pair in range(CELLS // 2):
+            both = source_ref[8 * pair : 8 * pair + 8, lanes]
+            swapped = pltpu.roll(both, 4, 0)
+            cells.append(jnp.where(low, both, swapped))
+            cells.append(jnp.where(low, swapped, both))
         for y in range(4):
-            for x in range(4):
-                total = None
-                for fy in range(4):
+            totals = [None, None]
+            for fy in range(4):
+                dy = (y - fy if back else fy - y) + 3
+                taps = [
+                    jnp.broadcast_to(kernel_ref[dy, dx : dx + 1, lanes], (8, 128)) for dx in range(7)
+                ]
+                if back:
+                    weights = {dx: jnp.where(low, taps[dx], taps[dx + 1]) for dx in range(6)}
+                else:
+                    weights = {dx: jnp.where(low, taps[dx], taps[dx - 1]) for dx in range(1, 7)}
+                for half in range(2):
                     for fx in range(4):
-                        dy, dx = (y - fy, x - fx) if back else (fy - y, fx - x)
-                        term = taps[dy + 3, dx + 3] * cells[fy * 4 + fx]
-                        total = term if total is None else total + term
-                place = 4 * (y * 4 + x)
-                out_ref[place : place + 4, lanes] = total[0:4]
+                        dx = (2 * half - fx if back else fx - 2 * half) + 3
+                        term = weights[dx] * cells[fy * 4 + fx]
+                        totals[half] = term if totals[half] is None else totals[half] + term
+            for half in range(2):
+                place = 16 * y + 8 * half
+                out_ref[place : place + 8, lanes] = totals[half]
 
 
 def step_kernel(
@@ -142,6 +142,7 @@
     gain_two_ref,
     inward_two_ref,
     outward_two_ref,
+    placing_ref,
     features_ref,
     grads_ref,
     taps_one,
@@ -156,7 +157,31 @@
     back_two,
     padded,
     spread,
+    cot_cells,
+    hidden_back,
+    patches_back,
+    inward,
+    outward,
+    placing,
+    inward_one,
+    outward_one,
+    project,
+    inward_two,
+    outward_two,
+    arrived,
 ):
+    copies = []
+    pairs = (
+        (placing_ref, placing),
+        (inward_one_ref, inward_one),
+        (outward_one_ref, outward_one),
+        (project_ref, project),
+        (inward_two_ref, inward_two),
+        (outward_two_ref, outward_two),
+    )
+    for index, (source, target) in enumerate(pairs):
+        copies.append(pltpu.make_async_copy(source, target, arrived.at[index]))
+        copies[-1].start()
     count = plan_ref[0, 0]
     kept = []
     for tile in range(TILES):
@@ -170,41 +195,51 @@
     gain_down = gain_down_ref[...].astype(F32).reshape(1, NARROW)
     gain_two = gain_two_ref[...].astype(F32).reshape(1, WIDE)
 
-    placing = one_hot((HIDDEN, HIDDEN), hidden_source, 1)
-    inward = product(inward_one_ref[...], placing).astype(BF16)
-    outward = product(outward_one_ref[...], placing).astype(BF16)
-
     for tile in range(TILES):
+        if tile == 2:
+            for copy in copies[:3]:
+                copy.wait()
+            inward[...] = product(inward_one[...], placing[...]).astype(BF16)
+            outward[...] = product(outward_one[...], placing[...]).astype(BF16)
         own = jnp.where(kept[tile], feats_ref[tile].astype(F32), 0.0)
         rows = slice(tile * 64, tile * 64 + 64)
         field[rows, :] = own.reshape(64, NARROW).astype(BF16)
         scaled, _ = statistics(conv_one(own, taps_one))
         normed_rows[rows, :] = (scaled * gain_one).astype(BF16)
 
+    for copy in copies[3:]:
+        copy.wait()
     gather_rows = one_hot((ROWS, ROWS), row_source, 0)
+    for index in range(CELLS):
+        tile, y = index // 4, index % 4
+        own = jnp.where(kept[tile], cot_ref[tile, y].astype(F32), 0.0)
+        cot_cells[4 * index : 4 * index + 4, :] = own
+    gather_cells = one_hot((ROWS_TWO, ROWS_TWO), cell_source, 0)
+    flat_cot = product(gather_cells, cot_cells[...].astype(BF16))
+    back_two[...] = product(flat_cot.astype(BF16), outward_two[...], (1, 1)).astype(BF16)
     normed = product(gather_rows, normed_rows[...]).astype(BF16)
     field_rows = product(gather_rows, field[...])
-    expand[...] = product(normed, inward)
-    gelu_rows(expand, hidden, 16)
-    section = (field_rows + product(hidden[...], outward, (1, 1))).astype(BF16).astype(F32)
+    gelu_columns(normed, inward, hidden, expand, 256)
+    hidden_back[...] = hidden[...].T
+    section = (field_rows + product(hidden[...], outward[...], (1, 1))).astype(BF16).astype(F32)
     scaled_down, scale_down = statistics(section)
     down = (scaled_down * gain_down).astype(BF16)
-    merged = None
+    merged = patches = None
     for block in range(4):
-        part = product(
-            down[block * 64 : block * 64 + 64], project_ref[block * NARROW : (block + 1) * NARROW, :]
-        )
+        rows = slice(block * NARROW, (block + 1) * NARROW)
+        own = down[block * 64 : block * 64 + 64]
+        part, place = product(own, project[rows, :]), product(own, placing[rows, :])
         merged = part if merged is None else merged + part
+        patches = place if patches is None else patches + place
+    patches_back[...] = patches.T.astype(BF16)
     merged = merged.astype(BF16).astype(F32)
 
-    padded[0:ROWS_TWO, :] = merged
-    padded[ROWS_TWO : ROWS_TWO + 8, :] = jnp.zeros((8, WIDE), F32)
+    padded[...] = merged
     conv_two(padded, taps_two, spread, False)
     scaled_two, scale_two = statistics(spread[...])
     normed_two = (scaled_two * gain_two).astype(BF16)
-    expand_two[...] = product(normed_two, inward_two_ref[...])
-    gelu_rows(expand_two, hidden_two, 16)
-    features = (merged + product(hidden_two[...], outward_two_ref[...])).astype(BF16)
+    gelu_columns(normed_two, inward_two, hidden_two, expand_two, 512)
+    features = (merged + product(hidden_two[...], outward_two[...])).astype(BF16)
     scatter_cells = one_hot((ROWS_TWO, ROWS_TWO), tile_place, 0)
     spread[...] = product(scatter_cells, features)
     for index in range(CELLS):
@@ -212,32 +247,24 @@
         own = spread[4 * index : 4 * index + 4, :]
         features_ref[tile, y] = jnp.where(kept[tile], own, 0.0).astype(BF16)
 
-    for index in range(CELLS):
-        tile, y = index // 4, index % 4
-        own = jnp.where(kept[tile], cot_ref[tile, y].astype(F32), 0.0)
-        spread[4 * index : 4 * index + 4, :] = own
-    gather_cells = one_hot((ROWS_TWO, ROWS_TWO), cell_source, 0)
-    flat_cot = product(gather_cells, spread[...].astype(BF16))
-    back_two[...] = product(flat_cot.astype(BF16), outward_two_ref[...], (1, 1)).astype(BF16)
-    slope_rows(expand_two, back_two, 16)
-    back_normed_two = product(back_two[...], inward_two_ref[...], (1, 1)).astype(BF16).astype(F32)
-    padded[0:ROWS_TWO, :] = norm_back(scaled_two, scale_two, back_normed_two * gain_two)
+    back_two[...] = (expand_two[...] * back_two[...].astype(F32)).astype(BF16)
+    back_normed_two = product(back_two[...], inward_two[...], (1, 1)).astype(BF16).astype(F32)
+    padded[...] = norm_back(scaled_two, scale_two, back_normed_two * gain_two)
     conv_two(padded, taps_two, spread, True)
     back_merged = (flat_cot + spread[...]).astype(BF16)
 
-    patches = None
     back_down = []
     for block in range(4):
         rows = slice(block * NARROW, (block + 1) * NARROW)
-        part = product(down[block * 64 : block * 64 + 64], placing[rows, :])
-        patches = part if patches is None else patches + part
-        back_down.append(product(back_merged, project_ref[rows, :], (1, 1)))
+        back_down.append(product(back_merged, project[rows, :], (1, 1)))
     back_down = jnp.concatenate(back_down, axis=0).astype(BF16).astype(F32)
-    grad_project = product(patches.astype(BF16), back_merged, (0, 0)).astype(BF16)
+    grad_project = product(patches_back[...], back_merged).astype(BF16)
     back_section = norm_back(scaled_down, scale_down, back_down * gain_down).astype(BF16)
-    back_hidden[...] = product(back_section, outward).astype(BF16)
-    slope_rows(expand, back_hidden, 16)
-    grad_outward = product(hidden[...], back_section, (0, 0)).astype(BF16)
+    for left in range(0, HIDDEN, 256):
+        columns = slice(left, left + 256)
+        back = product(back_section, outward[:, columns]).astype(BF16).astype(F32)
+        back_hidden[:, columns] = (expand[:, columns] * back).astype(BF16)
+    grad_outward = product(hidden_back[...], back_section).astype(BF16)
     grad_inward = product(back_hidden[...], normed, (0, 0)).astype(BF16)
     for third in range(3):
         for core in range(2):
@@ -251,9 +278,12 @@
 def local_step(*operands):
     smem = pl.BlockSpec(memory_space=pltpu.SMEM)
     vmem = pl.BlockSpec(memory_space=pltpu.VMEM)
+    hbm = pl.BlockSpec(memory_space=pl.ANY)
+    source = hidden_source(np.arange(HIDDEN))
+    placing = np.arange(HIDDEN)[:, None] == source[None, :]
     return pl.pallas_call(
         step_kernel,
-        in_specs=[smem, smem] + [vmem] * 12,
+        in_specs=[smem, smem] + [vmem] * 4 + [hbm, hbm, vmem, hbm, vmem, vmem, hbm, hbm, hbm],
         out_specs=[vmem, vmem],
         out_shape=[
             jax.ShapeDtypeStruct((TILES, 4, 4, WIDE), BF16),
@@ -270,39 +300,31 @@
             pltpu.VMEM((ROWS_TWO, HIDDEN_TWO), F32),
             pltpu.VMEM((ROWS_TWO, HIDDEN_TWO), BF16),
             pltpu.VMEM((ROWS_TWO, HIDDEN_TWO), BF16),
-            pltpu.VMEM((ROWS_TWO + 8, WIDE), F32),
             pltpu.VMEM((ROWS_TWO, WIDE), F32),
+            pltpu.VMEM((ROWS_TWO, WIDE), F32),
+            pltpu.VMEM((ROWS_TWO, WIDE), F32),
+            pltpu.VMEM((HIDDEN, ROWS), BF16),
+            pltpu.VMEM((HIDDEN, ROWS_TWO), BF16),
+            pltpu.VMEM((NARROW, HIDDEN), BF16),
+            pltpu.VMEM((NARROW, HIDDEN), BF16),
+            pltpu.VMEM((HIDDEN, HIDDEN), BF16),
+            pltpu.VMEM((NARROW, HIDDEN), BF16),
+            pltpu.VMEM((NARROW, HIDDEN), BF16),
+            pltpu.VMEM((HIDDEN, WIDE), BF16),
+            pltpu.VMEM((WIDE, HIDDEN_TWO), BF16),
+            pltpu.VMEM((HIDDEN_TWO, WIDE), BF16),
+            pltpu.SemaphoreType.DMA((6,)),
         ],
         name="local_step",
-    )(*operands)
-
-
-def spread_kernel(parts_ref, out_ref):
-    def step(index, carry):
-        rows = pl.ds(pl.multiple_of(index * 16, 16), 16)
-        total = parts_ref[0, rows, :].astype(F32)
-        for part in range(1, parts_ref.shape[0]):
-            total = total + parts_ref[part, rows, :].astype(F32)
-        for slide in range(8):
-            out_ref[index * 8 + slide] = total[2 * slide : 2 * slide + 2].astype(BF16)
-        return carry
-
-    lax.fori_loop(0, parts_ref.shape[1] // 16, step, 0)
-
-
-def spread_sum(parts):
-    vmem = pl.BlockSpec(memory_space=pltpu.VMEM)
-    return pl.pallas_call(
-        spread_kernel,
-        in_specs=[vmem],
-        out_specs=vmem,
-        out_shape=jax.ShapeDtypeStruct((parts.shape[1] // 2, 2, parts.shape[2]), BF16),
-        name="spread_sum",
-    )(parts)
+    )(*operands, jnp.asarray(placing, BF16))
 
 
 def exchange(pieces, axis):
     return lax.all_to_all(pieces, axis, split_axis=0, concat_axis=0, tiled=True)
+
+
+def summed(pieces, axis):
+    return exchange(pieces, axis).astype(F32).sum(axis=0)
 
 
 def per_device(
@@ -337,9 +359,9 @@
         inward_two,
         outward_two,
     )
-    own = exchange(grads, "core").astype(F32).sum(axis=0).astype(BF16)
-    own = spread_sum(exchange(own.reshape(4, 32, own.shape[1]), "x"))
-    own = exchange(own, "z").astype(F32).sum(axis=0)
+    own = summed(grads, "core").astype(BF16)
+    own = summed(own.reshape(4, 32, own.shape[1]), "x").astype(BF16)
+    own = summed(own.reshape(16, 2, own.shape[1]), "z")
     share = exchange(jnp.broadcast_to(own, (4, *own.shape)), "rep").sum(axis=0)
     share = share.reshape(2, 3, HIDDEN).transpose(1, 0, 2).reshape(6, HIDDEN)
     return (features, share[:, :NARROW].T, share[:, NARROW:WIDE], share[:, WIDE:])

time: 75.4 us -> 70.9 us (0.940)
  Pallas kernels: 13.2 us -> 8.99 us
    pallas_call x2 -> x1, Pallas kernels: 13.2 us -> 8.99 us  [local_step(): pl.pallas_call(step_kernel, in_specs=[smem, smem] + [vmem] * 4 + [hbm, hb...]
where the time goes in v4:
time: 70.9 us; the launch traced here: 69.8 us
  blocking collectives  58.1 us (82%)
  Pallas kernels  8.99 us (13%)
  local copies, waits for them, and re-layouts  1.41 us (2%)
    all_to_all x4, blocking collectives, exchange(): return lax.all_to_all(pieces, axis, split_axis=0, concat_axis=0, tiled=True)  58.1 us
    pallas_call x1, Pallas kernels, local_step(): pl.pallas_call(step_kernel, in_specs=[smem, smem] + [vmem] * 4 + [hbm, hb...  8.99 us

profile of v4, /device:TPU:6, one launch (start us, length us, event | category | flops | bytes accessed | tf_op | source)
XLA Modules:
  0.0 69.8 jit_solution(4726407064074924349)
XLA Ops:
  0.6 9.0 %local_step.1 = (bf16[4,4,4,384]{3,2,1,0:T(4,128)(2,1)}, bf16[2,128,2304]{2,1,0:T(8,128)(2,1)}) custom-call(s32[1,4]{1,0:T(1,128)} %keep_ref.1, s32[1,2]{1,0:T(1,128)} %plan_ref.1, bf16[4,8,8,192]{3,2,1,0:T(8,128)(2,1)} %feats_ref.1, bf16[4,4,4,384]{3,2,1,0:T(4,128)(2,1)} %cot_ref.1, bf16[7,7,192]{2,1,0:T(8,128)(2,1)} %kernel_one_ref.1, ...), custom_call_target="tpu_custom_call" | custom-call | tf_op jit(solution)/shard_map/local_step/pallas_call | solution.py:284
  9.6 5.8 %all_to_all.20 = bf16[2,128,2304]{2,1,0:T(8,128)(2,1)S(1)} all-to-all(bf16[2,128,2304]{2,1,0:T(8,128)(2,1)} %get-tuple-element.7), channel_id=1, replica_groups=mesh['x'=4,'z'=16,'core'=2,'rep'=4] {'core'}, dimensions={0} | all-to-all | bytes 2359296 | tf_op jit(solution)/shard_map/all_to_all | solution.py:323
  15.4 0.4 reduce_sum.42
  15.8 16.9 %all_to_all.21 = bf16[4,32,2304]{2,1,0:T(8,128)(2,1)S(1)} all-to-all(bf16[4,32,2304]{2,1,0:T(8,128)(2,1)S(1)} %bitcast.5), channel_id=1, replica_groups=mesh['x'=4,'z'=16,'core'=2,'rep'=4] {'x'}, dimensions={0} | all-to-all | bytes 1179648 | tf_op jit(solution)/shard_map/all_to_all | solution.py:323
  32.7 0.1 reduce_sum.43
  32.8 0.1 reshape.21
  32.9 25.5 %all_to_all.22 = bf16[16,2,2304]{2,1,0:T(2,128)(2,1)S(1)} all-to-all(bf16[16,2,2304]{2,1,0:T(2,128)(2,1)S(1)} %reshape.21), channel_id=1, replica_groups=mesh['x'=4,'z'=16,'core'=2,'rep'=4] {'z'}, dimensions={0} | all-to-all | bytes 294912 | tf_op jit(solution)/shard_map/all_to_all | solution.py:323
  58.4 0.1 convert_reduce_fusion
  58.4 9.9 %all_to_all.23 = f32[4,2,2304]{2,1,0:T(2,128)S(1)} all-to-all(f32[4,2,2304]{2,1,0:T(2,128)S(1)} %broadcast_in_dim.3), channel_id=1, replica_groups=mesh['x'=4,'z'=16,'core'=2,'rep'=4] {'rep'}, dimensions={0} | all-to-all | bytes 147456 | tf_op jit(solution)/shard_map/all_to_all | solution.py:323
  68.5 0.6 slice.14
  69.1 0.7 fusion
  (5 shorter events, 0.1 us)

commit v5 on v4

--- a/solution.py
+++ b/solution.py
@@ -46,12 +46,27 @@
     return values * below, below + values * (DENSITY * jnp.exp(-0.5 * values * values))
 
 
-def gelu_columns(rows, weights_ref, hidden_ref, slope_ref, block):
+def gelu_columns(rows, weights_ref, hidden_ref, slope_ref, block, fillers):
+    width = slope_ref.shape[1]
+    ahead = product(rows, weights_ref[:, :block])
+    for left in range(0, width, block):
+        own = ahead
+        if left + block < width:
+            ahead = product(rows, weights_ref[:, left + block : left + 2 * block])
+        run_next(fillers)
+        for top in range(0, slope_ref.shape[0], 32):
+            place = slice(top, top + 32), slice(left, left + block)
+            hidden, slope = gelu_parts(own[top : top + 32])
+            hidden_ref[place] = hidden.astype(BF16)
+            slope_ref[place] = slope
+
+
+def slope_columns(rows, weights_ref, slope_ref, back_ref, block):
     for left in range(0, slope_ref.shape[1], block):
-        columns = slice(left, left + block)
-        hidden, slope = gelu_parts(product(rows, weights_ref[:, columns]))
-        hidden_ref[:, columns] = hidden.astype(BF16)
-        slope_ref[:, columns] = slope
+        back = product(rows, weights_ref[:, left : left + block]).astype(BF16)
+        for top in range(0, slope_ref.shape[0], 64):
+            place = slice(top, top + 64), slice(left, left + block)
+            back_ref[place] = (slope_ref[place] * back[top : top + 64].astype(F32)).astype(BF16)
 
 
 def one_hot(shape, source, source_dim):
@@ -60,9 +75,9 @@
     return jnp.where(own == source(index), 1.0, 0.0).astype(BF16)
 
 
-def hidden_source(place):
+def hidden_source(place, mine):
     third, rest = place >> 8, place & 255
-    core, pair, low = rest >> 7, (rest >> 1) & 63, rest & 1
+    core, pair, low = (rest >> 7) ^ mine, (rest >> 1) & 63, rest & 1
     return (pair * 2 + core) * 6 + third * 2 + low
 
 
@@ -80,7 +95,12 @@
     return (place & 15) * 4 + (place >> 4)
 
 
-def conv_one(tile, kernel_ref):
+def run_next(fillers):
+    if fillers:
+        fillers.pop(0)()
+
+
+def conv_one(tile, kernel_ref, fillers):
     cell = lax.broadcasted_iota(jnp.int32, (8, NARROW), 0)
     sums = [None] * 8
     for dx in range(-3, 4):
@@ -93,10 +113,11 @@
             for target in range(max(0, source - 3), min(8, source + 4)):
                 term = taps[source - target + 3] * line
                 sums[target] = term if sums[target] is None else sums[target] + term
+        run_next(fillers)
     return jnp.concatenate(sums, axis=0)
 
 
-def conv_two(source_ref, kernel_ref, out_ref, back):
+def conv_two(source_ref, kernel_ref, out_ref, back, fillers):
     low = lax.broadcasted_iota(jnp.int32, (8, 128), 0) < 4
     for part in range(WIDE // 128):
         lanes = slice(part * 128, part * 128 + 128)
@@ -125,6 +146,7 @@
             for half in range(2):
                 place = 16 * y + 8 * half
                 out_ref[place : place + 8, lanes] = totals[half]
+            run_next(fillers)
 
 
 def step_kernel(
@@ -144,7 +166,8 @@
     outward_two_ref,
     placing_ref,
     features_ref,
-    grads_ref,
+    mine_ref,
+    theirs_ref,
     taps_one,
     taps_two,
     field,
@@ -172,7 +195,7 @@
 ):
     copies = []
     pairs = (
-        (placing_ref, placing),
+        (placing_ref.at[lax.axis_index("core")], placing),
         (inward_one_ref, inward_one),
         (outward_one_ref, outward_one),
         (project_ref, project),
@@ -195,99 +218,135 @@
     gain_down = gain_down_ref[...].astype(F32).reshape(1, NARROW)
     gain_two = gain_two_ref[...].astype(F32).reshape(1, WIDE)
 
+    fillers = []
+
+    def place_columns(source, target, left):
+        columns = slice(left, left + 256)
+        target[:, columns] = product(source[...], placing[:, columns]).astype(BF16)
+
     for tile in range(TILES):
         if tile == 2:
             for copy in copies[:3]:
                 copy.wait()
-            inward[...] = product(inward_one[...], placing[...]).astype(BF16)
-            outward[...] = product(outward_one[...], placing[...]).astype(BF16)
+            for left in range(0, HIDDEN, 256):
+                fillers.append(lambda left=left: place_columns(inward_one, inward, left))
+            for left in range(0, HIDDEN, 256):
+                fillers.append(lambda left=left: place_columns(outward_one, outward, left))
         own = jnp.where(kept[tile], feats_ref[tile].astype(F32), 0.0)
         rows = slice(tile * 64, tile * 64 + 64)
         field[rows, :] = own.reshape(64, NARROW).astype(BF16)
-        scaled, _ = statistics(conv_one(own, taps_one))
+        scaled, _ = statistics(conv_one(own, taps_one, fillers))
         normed_rows[rows, :] = (scaled * gain_one).astype(BF16)
 
-    for copy in copies[3:]:
-        copy.wait()
-    gather_rows = one_hot((ROWS, ROWS), row_source, 0)
     for index in range(CELLS):
         tile, y = index // 4, index % 4
         own = jnp.where(kept[tile], cot_ref[tile, y].astype(F32), 0.0)
         cot_cells[4 * index : 4 * index + 4, :] = own
+    for copy in copies[3:]:
+        copy.wait()
+    gather_rows = one_hot((ROWS, ROWS), row_source, 0)
+    normed = product(gather_rows, normed_rows[...]).astype(BF16)
     gather_cells = one_hot((ROWS_TWO, ROWS_TWO), cell_source, 0)
     flat_cot = product(gather_cells, cot_cells[...].astype(BF16))
-    back_two[...] = product(flat_cot.astype(BF16), outward_two[...], (1, 1)).astype(BF16)
-    normed = product(gather_rows, normed_rows[...]).astype(BF16)
+    cot_rows = flat_cot.astype(BF16)
+
+    def cot_columns(left):
+        columns = slice(left, left + 512)
+        back_two[:, columns] = product(cot_rows, outward_two[columns, :], (1, 1)).astype(BF16)
+
+    fillers = [lambda left=left: cot_columns(left) for left in range(0, HIDDEN_TWO, 512)]
+    gelu_columns(normed, inward, hidden, expand, 256, fillers)
     field_rows = product(gather_rows, field[...])
-    gelu_columns(normed, inward, hidden, expand, 256)
-    hidden_back[...] = hidden[...].T
     section = (field_rows + product(hidden[...], outward[...], (1, 1))).astype(BF16).astype(F32)
-    scaled_down, scale_down = statistics(section)
-    down = (scaled_down * gain_down).astype(BF16)
-    merged = patches = None
+    merged = None
+    down, scaled_down, scale_down = [], [], []
     for block in range(4):
         rows = slice(block * NARROW, (block + 1) * NARROW)
-        own = down[block * 64 : block * 64 + 64]
-        part, place = product(own, project[rows, :]), product(own, placing[rows, :])
+        scaled, scale = statistics(section[block * 64 : block * 64 + 64])
+        scaled_down.append(scaled)
+        scale_down.append(scale)
+        down.append((scaled * gain_down).astype(BF16))
+        part = product(down[block], project[rows, :])
         merged = part if merged is None else merged + part
-        patches = place if patches is None else patches + place
-    patches_back[...] = patches.T.astype(BF16)
     merged = merged.astype(BF16).astype(F32)
 
+    def place_patches(left):
+        columns = slice(left, left + 256)
+        total = None
+        for block in range(4):
+            part = product(down[block], placing[block * NARROW : (block + 1) * NARROW, columns])
+            total = part if total is None else total + part
+        patches_back[columns, :] = total.T.astype(BF16)
+
+    def turn_hidden(left):
+        columns = slice(left, left + 256)
+        hidden_back[columns, :] = hidden[:, columns].T
+
+    fillers = []
+    for left in range(0, HIDDEN, 256):
+        fillers.append(lambda left=left: place_patches(left))
+        fillers.append(lambda left=left: turn_hidden(left))
     padded[...] = merged
-    conv_two(padded, taps_two, spread, False)
+    conv_two(padded, taps_two, spread, False, fillers)
     scaled_two, scale_two = statistics(spread[...])
     normed_two = (scaled_two * gain_two).astype(BF16)
-    gelu_columns(normed_two, inward_two, hidden_two, expand_two, 512)
-    features = (merged + product(hidden_two[...], outward_two[...])).astype(BF16)
+    gelu_columns(normed_two, inward_two, hidden_two, expand_two, 512, [])
+    for left in range(0, HIDDEN_TWO, 512):
+        columns = slice(left, left + 512)
+        back_two[:, columns] = (expand_two[:, columns] * back_two[:, columns].astype(F32)).astype(BF16)
+    back_normed_two = product(back_two[...], inward_two[...], (1, 1)).astype(BF16).astype(F32)
+
+    def feature_columns(left):
+        columns = slice(left, left + 128)
+        own = product(hidden_two[...], outward_two[:, columns])
+        cot_cells[:, columns] = merged[:, columns] + own
+
+    fillers = [lambda left=left: feature_columns(left) for left in range(0, WIDE, 128)]
+    padded[...] = norm_back(scaled_two, scale_two, back_normed_two * gain_two)
+    conv_two(padded, taps_two, spread, True, fillers)
+    back_merged = (flat_cot + spread[...]).astype(BF16)
+
+    back_section = []
+    for block in range(4):
+        rows = slice(block * NARROW, (block + 1) * NARROW)
+        back = product(back_merged, project[rows, :], (1, 1)).astype(BF16).astype(F32)
+        back = norm_back(scaled_down[block], scale_down[block], back * gain_down)
+        back_section.append(back.astype(BF16))
+    back_section = jnp.concatenate(back_section, axis=0)
+    slope_columns(back_section, outward, expand, back_hidden, 256)
     scatter_cells = one_hot((ROWS_TWO, ROWS_TWO), tile_place, 0)
-    spread[...] = product(scatter_cells, features)
+    spread[...] = product(scatter_cells, cot_cells[...].astype(BF16))
+    for third in range(3):
+        hiddens = slice(third * 256, third * 256 + 256)
+        left = third * HIDDEN
+        grad_project = product(patches_back[hiddens, :], back_merged).astype(BF16)
+        grad_outward = product(hidden_back[hiddens, :], back_section).astype(BF16)
+        grad_inward = product(back_hidden[:, hiddens], normed, (0, 0)).astype(BF16)
+        for core, grads_ref in enumerate((mine_ref, theirs_ref)):
+            rows = slice(core * 128, core * 128 + 128)
+            grads_ref[:, left : left + NARROW] = grad_inward[rows]
+            grads_ref[:, left + NARROW : left + WIDE] = grad_outward[rows]
+            grads_ref[:, left + WIDE : left + HIDDEN] = grad_project[rows]
     for index in range(CELLS):
         tile, y = index // 4, index % 4
         own = spread[4 * index : 4 * index + 4, :]
         features_ref[tile, y] = jnp.where(kept[tile], own, 0.0).astype(BF16)
 
-    back_two[...] = (expand_two[...] * back_two[...].astype(F32)).astype(BF16)
-    back_normed_two = product(back_two[...], inward_two[...], (1, 1)).astype(BF16).astype(F32)
-    padded[...] = norm_back(scaled_two, scale_two, back_normed_two * gain_two)
-    conv_two(padded, taps_two, spread, True)
-    back_merged = (flat_cot + spread[...]).astype(BF16)
-
-    back_down = []
-    for block in range(4):
-        rows = slice(block * NARROW, (block + 1) * NARROW)
-        back_down.append(product(back_merged, project[rows, :], (1, 1)))
-    back_down = jnp.concatenate(back_down, axis=0).astype(BF16).astype(F32)
-    grad_project = product(patches_back[...], back_merged).astype(BF16)
-    back_section = norm_back(scaled_down, scale_down, back_down * gain_down).astype(BF16)
-    for left in range(0, HIDDEN, 256):
-        columns = slice(left, left + 256)
-        back = product(back_section, outward[:, columns]).astype(BF16).astype(F32)
-        back_hidden[:, columns] = (expand[:, columns] * back).astype(BF16)
-    grad_outward = product(hidden_back[...], back_section).astype(BF16)
-    grad_inward = product(back_hidden[...], normed, (0, 0)).astype(BF16)
-    for third in range(3):
-        for core in range(2):
-            rows = slice(third * 256 + core * 128, third * 256 + core * 128 + 128)
-            left = third * HIDDEN
-            grads_ref[core, :, left : left + NARROW] = grad_inward[rows]
-            grads_ref[core, :, left + NARROW : left + WIDE] = grad_outward[rows]
-            grads_ref[core, :, left + WIDE : left + HIDDEN] = grad_project[rows]
-
 
 def local_step(*operands):
     smem = pl.BlockSpec(memory_space=pltpu.SMEM)
     vmem = pl.BlockSpec(memory_space=pltpu.VMEM)
     hbm = pl.BlockSpec(memory_space=pl.ANY)
-    source = hidden_source(np.arange(HIDDEN))
-    placing = np.arange(HIDDEN)[:, None] == source[None, :]
+    place = np.arange(HIDDEN)
+    placing = np.stack([place[:, None] == hidden_source(place, mine)[None, :] for mine in (0, 1)])
     return pl.pallas_call(
         step_kernel,
         in_specs=[smem, smem] + [vmem] * 4 + [hbm, hbm, vmem, hbm, vmem, vmem, hbm, hbm, hbm],
-        out_specs=[vmem, vmem],
+        out_specs=[vmem, vmem, vmem],
         out_shape=[
             jax.ShapeDtypeStruct((TILES, 4, 4, WIDE), BF16),
-            jax.ShapeDtypeStruct((2, 128, 3 * HIDDEN), BF16),
+            jax.ShapeDtypeStruct((128, 3 * HIDDEN), BF16),
+            jax.ShapeDtypeStruct((128, 3 * HIDDEN), BF16),
         ],
         scratch_shapes=[
             pltpu.VMEM((7, 7, NARROW), F32),
@@ -343,7 +402,7 @@
     inward_two,
     outward_two,
 ):
-    features, grads = local_step(
+    features, mine, theirs = local_step(
         keep_list,
         tile_plan,
         tile_feats,
@@ -359,7 +418,8 @@
         inward_two,
         outward_two,
     )
-    own = summed(grads, "core").astype(BF16)
+    arrived = lax.ppermute(theirs, "core", [(0, 1), (1, 0)])
+    own = (mine.astype(F32) + arrived.astype(F32)).astype(BF16)
     own = summed(own.reshape(4, 32, own.shape[1]), "x").astype(BF16)
     own = summed(own.reshape(16, 2, own.shape[1]), "z")
     share = exchange(jnp.broadcast_to(own, (4, *own.shape)), "rep").sum(axis=0)

time: 70.9 us -> 69.5 us (0.980)
  blocking collectives: 58.1 us -> 52.3 us
  waiting for transfers between devices: 0 us -> 2.18 us
  starting transfers between devices: 0 us -> 1.92 us
  other arithmetic: 0.55 us -> 1.39 us
    all_to_all x4 -> x3, blocking collectives: 58.1 us -> 52.3 us  [exchange(): return lax.all_to_all(pieces, axis, split_axis=0, concat_axis=0, tiled=True)]
    ppermute x0 -> x1, waiting for transfers between devices: none -> 2.18 us  [per_device(): arrived = lax.ppermute(theirs, 'core', [(0, 1), (1, 0)])]
    ppermute x0 -> x1, starting transfers between devices: none -> 1.92 us  [per_device(): arrived = lax.ppermute(theirs, 'core', [(0, 1), (1, 0)])]
    convert_element_type x0 -> x1, other arithmetic: none -> 1.2 us  [per_device(): own = (mine.astype(F32) + arrived.astype(F32)).astype(BF16)]
  transfers between devices with their start and end apart: 0 -> 1, of which waited for: 0 -> 1; matrix products, arithmetic and copies ran while one was open for 0% -> 0% of each run, Pallas kernels for 0% -> 0%
where the time goes in v5:
time: 69.5 us; the launch traced here: 68.3 us
  blocking collectives  52.3 us (75%)
  Pallas kernels  8.39 us (12%)
  waiting for transfers between devices  2.18 us (3%)
  starting transfers between devices  1.92 us (3%)
  local copies, waits for them, and re-layouts  1.41 us (2%)
  other arithmetic  1.39 us (2%)
    all_to_all x3, blocking collectives, exchange(): return lax.all_to_all(pieces, axis, split_axis=0, concat_axis=0, tiled=True)  52.3 us
    pallas_call x1, Pallas kernels, local_step(): pl.pallas_call(step_kernel, in_specs=[smem, smem] + [vmem] * 4 + [hbm, hb...  8.39 us
    ppermute x1, waiting for transfers between devices, per_device(): arrived = lax.ppermute(theirs, 'core', [(0, 1), (1, 0)])  2.18 us
    ppermute x1, starting transfers between devices, per_device(): arrived = lax.ppermute(theirs, 'core', [(0, 1), (1, 0)])  1.92 us
  transfers between devices with their start and end apart: 1, of which 1 were waited for; matrix products, arithmetic and copies ran while one was open for 0% of the time, Pallas kernels for 0%

profile of v5, /device:TPU:6, one launch (start us, length us, event | category | flops | bytes accessed | tf_op | source)
XLA Modules:
  0.0 68.3 jit_solution(3629664832003008888)
XLA Ops:
  0.6 8.4 %local_step.1 = (bf16[4,4,4,384]{3,2,1,0:T(4,128)(2,1)}, bf16[128,2304]{1,0:T(8,128)(2,1)}, bf16[128,2304]{1,0:T(8,128)(2,1)}) custom-call(s32[1,4]{1,0:T(1,128)} %keep_ref.1, s32[1,2]{1,0:T(1,128)} %plan_ref.1, bf16[4,8,8,192]{3,2,1,0:T(8,128)(2,1)} %feats_ref.1, bf16[4,4,4,384]{3,2,1,0:T(4,128)(2,1)} %cot_ref.1, bf16[7,7,192]{2,1,0:T(8,128)(2,1)} %kernel_one_ref.1, ...), custom_call_target="tpu_custom_call" | custom-call | tf_op jit(solution)/shard_map/local_step/pallas_call | solution.py:342
  9.0 1.9 %collective-permute-start = (bf16[128,2304]{1,0:T(8,128)(2,1)}, bf16[128,2304]{1,0:T(8,128)(2,1)S(1)}, u32[]{:S(2)}, u32[]{:S(2)}) collective-permute-start(bf16[128,2304]{1,0:T(8,128)(2,1)} %get-tuple-element.9), channel_id=1, source_target_pairs={{0,4},{4,0},{1,5},{5,1},{2,6},{6,2},{3,7},{7,3},{8,12},{12,8},{9,1... | collective-permute-start | bytes 1769480 | tf_op jit(solution)/shard_map/ppermute | solution.py:421
  11.0 2.2 %collective-permute-done = bf16[128,2304]{1,0:T(8,128)(2,1)S(1)} collective-permute-done((bf16[128,2304]{1,0:T(8,128)(2,1)}, bf16[128,2304]{1,0:T(8,128)(2,1)S(1)}, u32[]{:S(2)}, u32[]{:S(2)}) %collective-permute-start) | collective-permute-done | bytes 589856 | tf_op jit(solution)/shard_map/ppermute | solution.py:421
  13.1 1.2 %add_convert_fusion = bf16[128,2304]{1,0:T(8,128)(2,1)S(1)} fusion(bf16[128,2304]{1,0:T(8,128)(2,1)S(1)} %collective-permute-done, bf16[128,2304]{1,0:T(8,128)(2,1)} %get-tuple-element.8), kind=kLoop, calls=%fused_computation | loop fusion | flops 1179648 | bytes 1769472 | tf_op jit(solution)/shard_map/convert_element_type | solution.py:422
  14.3 16.9 %all_to_all.15 = bf16[4,32,2304]{2,1,0:T(8,128)(2,1)S(1)} all-to-all(bf16[4,32,2304]{2,1,0:T(8,128)(2,1)S(1)} %bitcast.5), channel_id=1, replica_groups=mesh['x'=4,'z'=16,'core'=2,'rep'=4] {'x'}, dimensions={0} | all-to-all | bytes 1179648 | tf_op jit(solution)/shard_map/all_to_all | solution.py:382
  31.2 0.1 reduce_sum.30
  31.3 0.1 reshape.21
  31.4 25.5 %all_to_all.16 = bf16[16,2,2304]{2,1,0:T(2,128)(2,1)S(1)} all-to-all(bf16[16,2,2304]{2,1,0:T(2,128)(2,1)S(1)} %reshape.21), channel_id=1, replica_groups=mesh['x'=4,'z'=16,'core'=2,'rep'=4] {'z'}, dimensions={0} | all-to-all | bytes 294912 | tf_op jit(solution)/shard_map/all_to_all | solution.py:382
  56.9 0.1 convert_reduce_fusion
  57.0 9.9 %all_to_all.17 = f32[4,2,2304]{2,1,0:T(2,128)S(1)} all-to-all(f32[4,2,2304]{2,1,0:T(2,128)S(1)} %broadcast_in_dim.3), channel_id=1, replica_groups=mesh['x'=4,'z'=16,'core'=2,'rep'=4] {'rep'}, dimensions={0} | all-to-all | bytes 147456 | tf_op jit(solution)/shard_map/all_to_all | solution.py:382
  67.0 0.6 slice.14
  67.6 0.7 fusion
  (5 shorter events, 0.1 us)
Async XLA Ops:
  9.0 4.1 %collective-permute-start = (bf16[128,2304]{1,0:T(8,128)(2,1)}, bf16[128,2304]{1,0:T(8,128)(2,1)S(1)}, u32[]{:S(2)}, u32[]{:S(2)}) collective-permute-start(bf16[128,2304]{1,0:T(8,128)(2,1)} %get-tuple-element.9), channel_id=1, source_target_pairs={{0,4},{4,0},{1,5},{5,1},{2,6},{6,2},{3,7},{7,3},{8,12},{12,8},{9,1... | collective-permute-start | bytes 1769480 | tf_op jit(solution)/shard_map/ppermute | solution.py:421

commit v6 on v5

--- a/solution.py
+++ b/solution.py
@@ -345,8 +345,8 @@
         out_specs=[vmem, vmem, vmem],
         out_shape=[
             jax.ShapeDtypeStruct((TILES, 4, 4, WIDE), BF16),
-            jax.ShapeDtypeStruct((128, 3 * HIDDEN), BF16),
-            jax.ShapeDtypeStruct((128, 3 * HIDDEN), BF16),
+            pltpu.VMEM((128, 3 * HIDDEN), BF16),
+            pltpu.VMEM((128, 3 * HIDDEN), BF16),
         ],
         scratch_shapes=[
             pltpu.VMEM((7, 7, NARROW), F32),
@@ -376,6 +376,27 @@
         ],
         name="local_step",
     )(*operands, jnp.asarray(placing, BF16))
+
+
+def finish_kernel(parts_ref, inward_ref, outward_ref, project_ref):
+    total = parts_ref[0] + parts_ref[1] + parts_ref[2] + parts_ref[3]
+    for third in range(3):
+        left = third * HIDDEN
+        rows = slice(2 * third, 2 * third + 2)
+        inward_ref[rows, :] = total[:, left : left + NARROW]
+        outward_ref[rows, :] = total[:, left + NARROW : left + WIDE]
+        project_ref[rows, :] = total[:, left + WIDE : left + HIDDEN]
+
+
+def finish(parts):
+    vmem = pl.BlockSpec(memory_space=pltpu.VMEM)
+    return pl.pallas_call(
+        finish_kernel,
+        in_specs=[vmem],
+        out_specs=[vmem, vmem, vmem],
+        out_shape=[jax.ShapeDtypeStruct((6, width), F32) for width in (NARROW, NARROW, WIDE)],
+        name="finish",
+    )(pltpu.with_memory_space_constraint(parts, pltpu.VMEM))
 
 
 def exchange(pieces, axis):
@@ -422,9 +443,8 @@
     own = (mine.astype(F32) + arrived.astype(F32)).astype(BF16)
     own = summed(own.reshape(4, 32, own.shape[1]), "x").astype(BF16)
     own = summed(own.reshape(16, 2, own.shape[1]), "z")
-    share = exchange(jnp.broadcast_to(own, (4, *own.shape)), "rep").sum(axis=0)
-    share = share.reshape(2, 3, HIDDEN).transpose(1, 0, 2).reshape(6, HIDDEN)
-    return (features, share[:, :NARROW].T, share[:, NARROW:WIDE], share[:, WIDE:])
+    inward, outward, project = finish(exchange(jnp.broadcast_to(own, (4, *own.shape)), "rep"))
+    return (features, inward.T, outward, project)
 
 
 def solution(mesh):

time: 69.5 us -> 66.6 us (0.958)
  local copies, waits for them, and re-layouts: 1.41 us -> 0.08 us
  other arithmetic: 1.39 us -> 0.29 us
    slice x2 -> x0, local copies, waits for them, and re-layouts: 1.27 us -> none  [the longest x1 0.67 us: per_device(): share[:, NARROW:WIDE]]
    convert_element_type x1, other arithmetic: 1.2 us -> 0.14 us  [per_device(): own = (mine.astype(F32) + arrived.astype(F32)).astype(BF16)]
    pallas_call x1, Pallas kernels: 8.39 us -> 7.51 us  [local_step(): pl.pallas_call(step_kernel, in_specs=[smem, smem] + [vmem] * 4 + [hbm, hb...]
where the time goes in v6:
time: 66.6 us; the launch traced here: 65.4 us
  blocking collectives  52.3 us (79%)
  Pallas kernels  8.19 us (12%)
  waiting for transfers between devices  1.97 us (3%)
  starting transfers between devices  1.92 us (3%)
  between operations  0.67 us (1%)
    all_to_all x3, blocking collectives, exchange(): return lax.all_to_all(pieces, axis, split_axis=0, concat_axis=0, tiled=True)  52.3 us
    pallas_call x1, Pallas kernels, local_step(): pl.pallas_call(step_kernel, in_specs=[smem, smem] + [vmem] * 4 + [hbm, hb...  7.51 us
    ppermute x1, waiting for transfers between devices, per_device(): arrived = lax.ppermute(theirs, 'core', [(0, 1), (1, 0)])  1.97 us
    ppermute x1, starting transfers between devices, per_device(): arrived = lax.ppermute(theirs, 'core', [(0, 1), (1, 0)])  1.92 us
  transfers between devices with their start and end apart: 1, of which 1 were waited for; matrix products, arithmetic and copies ran while one was open for 0% of the time, Pallas kernels for 0%

profile of v6, /device:TPU:6, one launch (start us, length us, event | category | flops | bytes accessed | tf_op | source)
XLA Modules:
  0.0 65.4 jit_solution(74216628537976697)
XLA Ops:
  0.6 7.5 %local_step.1 = (bf16[4,4,4,384]{3,2,1,0:T(4,128)(2,1)}, bf16[128,2304]{1,0:T(8,128)(2,1)S(1)}, bf16[128,2304]{1,0:T(8,128)(2,1)S(1)}) custom-call(s32[1,4]{1,0:T(1,128)} %keep_ref.1, s32[1,2]{1,0:T(1,128)} %plan_ref.1, bf16[4,8,8,192]{3,2,1,0:T(8,128)(2,1)} %feats_ref.1, bf16[4,4,4,384]{3,2,1,0:T(4,128)(2,1)} %cot_ref.1, bf16[7,7,192]{2,1,0:T(8,128)(2,1)} %kernel_one_ref.1, ...), custom_call_target="tpu_custom_call" | custom-call | tf_op jit(solution)/shard_map/local_step/pallas_call | solution.py:342
  8.2 1.9 %collective-permute-start = (bf16[128,2304]{1,0:T(8,128)(2,1)S(1)}, bf16[128,2304]{1,0:T(8,128)(2,1)S(1)}, u32[]{:S(2)}, u32[]{:S(2)}) collective-permute-start(bf16[128,2304]{1,0:T(8,128)(2,1)S(1)} %get-tuple-element.12), channel_id=1, source_target_pairs={{0,4},{4,0},{1,5},{5,1},{2,6},{6,2},{3,7},{7,3},{8,12},{12,8},{9,1... | collective-permute-start | bytes 1769480 | tf_op jit(solution)/shard_map/ppermute | solution.py:442
  10.1 2.0 %collective-permute-done = bf16[128,2304]{1,0:T(8,128)(2,1)S(1)} collective-permute-done((bf16[128,2304]{1,0:T(8,128)(2,1)S(1)}, bf16[128,2304]{1,0:T(8,128)(2,1)S(1)}, u32[]{:S(2)}, u32[]{:S(2)}) %collective-permute-start) | collective-permute-done | bytes 589856 | tf_op jit(solution)/shard_map/ppermute | solution.py:442
  12.0 0.1 add_convert_fusion
  12.2 16.9 %all_to_all.15 = bf16[4,32,2304]{2,1,0:T(8,128)(2,1)S(1)} all-to-all(bf16[4,32,2304]{2,1,0:T(8,128)(2,1)S(1)} %bitcast.3), channel_id=1, replica_groups=mesh['x'=4,'z'=16,'core'=2,'rep'=4] {'x'}, dimensions={0} | all-to-all | bytes 1179648 | tf_op jit(solution)/shard_map/all_to_all | solution.py:403
  29.1 0.1 reduce_sum.21
  29.2 0.1 reshape.15
  29.3 25.5 %all_to_all.16 = bf16[16,2,2304]{2,1,0:T(2,128)(2,1)S(1)} all-to-all(bf16[16,2,2304]{2,1,0:T(2,128)(2,1)S(1)} %reshape.15), channel_id=1, replica_groups=mesh['x'=4,'z'=16,'core'=2,'rep'=4] {'z'}, dimensions={0} | all-to-all | bytes 294912 | tf_op jit(solution)/shard_map/all_to_all | solution.py:403
  54.7 0.1 convert_reduce_fusion
  54.8 9.9 %all_to_all.17.parts_ref = f32[4,2,2304]{2,1,0:T(2,128)S(1)} all-to-all(f32[4,2,2304]{2,1,0:T(2,128)S(1)} %broadcast_in_dim.3), channel_id=1, replica_groups=mesh['x'=4,'z'=16,'core'=2,'rep'=4] {'rep'}, dimensions={0} | all-to-all | bytes 147456 | tf_op jit(solution)/shard_map/all_to_all | solution.py:403
  64.8 0.7 %finish.1 = (f32[6,192]{1,0:T(8,128)}, f32[6,192]{1,0:T(8,128)}, f32[6,384]{1,0:T(8,128)}) custom-call(f32[4,2,2304]{2,1,0:T(2,128)S(1)} %all_to_all.17.parts_ref), custom_call_target="tpu_custom_call" | custom-call | tf_op jit(solution)/shard_map/finish/pallas_call | solution.py:393
  (1 shorter events, 0.0 us)
Async XLA Ops:
  8.2 3.9 %collective-permute-start = (bf16[128,2304]{1,0:T(8,128)(2,1)S(1)}, bf16[128,2304]{1,0:T(8,128)(2,1)S(1)}, u32[]{:S(2)}, u32[]{:S(2)}) collective-permute-start(bf16[128,2304]{1,0:T(8,128)(2,1)S(1)} %get-tuple-element.12), channel_id=1, source_target_pairs={{0,4},{4,0},{1,5},{5,1},{2,6},{6,2},{3,7},{7,3},{8,12},{12,8},{9,1... | collective-permute-start | bytes 1769480 | tf_op jit(solution)/shard_map/ppermute | solution.py:442

commit v7 on v6

--- a/solution.py
+++ b/solution.py
@@ -54,9 +54,9 @@
         if left + block < width:
             ahead = product(rows, weights_ref[:, left + block : left + 2 * block])
         run_next(fillers)
-        for top in range(0, slope_ref.shape[0], 32):
-            place = slice(top, top + 32), slice(left, left + block)
-            hidden, slope = gelu_parts(own[top : top + 32])
+        for top in range(0, slope_ref.shape[0], 64):
+            place = slice(top, top + 64), slice(left, left + block)
+            hidden, slope = gelu_parts(own[top : top + 64])
             hidden_ref[place] = hidden.astype(BF16)
             slope_ref[place] = slope
 
@@ -379,7 +379,9 @@
 
 
 def finish_kernel(parts_ref, inward_ref, outward_ref, project_ref):
-    total = parts_ref[0] + parts_ref[1] + parts_ref[2] + parts_ref[3]
+    total = parts_ref[0].astype(F32)
+    for part in range(1, 4):
+        total = total + parts_ref[part].astype(F32)
     for third in range(3):
         left = third * HIDDEN
         rows = slice(2 * third, 2 * third + 2)
@@ -442,7 +444,7 @@
     arrived = lax.ppermute(theirs, "core", [(0, 1), (1, 0)])
     own = (mine.astype(F32) + arrived.astype(F32)).astype(BF16)
     own = summed(own.reshape(4, 32, own.shape[1]), "x").astype(BF16)
-    own = summed(own.reshape(16, 2, own.shape[1]), "z")
+    own = summed(own.reshape(16, 2, own.shape[1]), "z").astype(BF16)
     inward, outward, project = finish(exchange(jnp.broadcast_to(own, (4, *own.shape)), "rep"))
     return (features, inward.T, outward, project)
 

time: 66.6 us -> 66.4 us (level)
  no operation moved by 1% of the time
where the time goes in v7:
time: 66.4 us; the launch traced here: 65.3 us
  blocking collectives  52.1 us (78%)
  Pallas kernels  8.19 us (12%)
  waiting for transfers between devices  1.97 us (3%)
  starting transfers between devices  1.92 us (3%)
  between operations  0.67 us (1%)
    all_to_all x3, blocking collectives, exchange(): return lax.all_to_all(pieces, axis, split_axis=0, concat_axis=0, tiled=True)  52.1 us
    pallas_call x1, Pallas kernels, local_step(): pl.pallas_call(step_kernel, in_specs=[smem, smem] + [vmem] * 4 + [hbm, hb...  7.51 us
    ppermute x1, waiting for transfers between devices, per_device(): arrived = lax.ppermute(theirs, 'core', [(0, 1), (1, 0)])  1.97 us
    ppermute x1, starting transfers between devices, per_device(): arrived = lax.ppermute(theirs, 'core', [(0, 1), (1, 0)])  1.92 us
  transfers between devices with their start and end apart: 1, of which 1 were waited for; matrix products, arithmetic and copies ran while one was open for 0% of the time, Pallas kernels for 0%

profile of v7, /device:TPU:6, one launch (start us, length us, event | category | flops | bytes accessed | tf_op | source)
XLA Modules:
  0.0 65.3 jit_solution(12119397577573236873)
XLA Ops:
  0.6 7.5 %local_step.1 = (bf16[4,4,4,384]{3,2,1,0:T(4,128)(2,1)}, bf16[128,2304]{1,0:T(8,128)(2,1)S(1)}, bf16[128,2304]{1,0:T(8,128)(2,1)S(1)}) custom-call(s32[1,4]{1,0:T(1,128)} %keep_ref.1, s32[1,2]{1,0:T(1,128)} %plan_ref.1, bf16[4,8,8,192]{3,2,1,0:T(8,128)(2,1)} %feats_ref.1, bf16[4,4,4,384]{3,2,1,0:T(4,128)(2,1)} %cot_ref.1, bf16[7,7,192]{2,1,0:T(8,128)(2,1)} %kernel_one_ref.1, ...), custom_call_target="tpu_custom_call" | custom-call | tf_op jit(solution)/shard_map/local_step/pallas_call | solution.py:342
  8.2 1.9 %collective-permute-start = (bf16[128,2304]{1,0:T(8,128)(2,1)S(1)}, bf16[128,2304]{1,0:T(8,128)(2,1)S(1)}, u32[]{:S(2)}, u32[]{:S(2)}) collective-permute-start(bf16[128,2304]{1,0:T(8,128)(2,1)S(1)} %get-tuple-element.12), channel_id=1, source_target_pairs={{0,4},{4,0},{1,5},{5,1},{2,6},{6,2},{3,7},{7,3},{8,12},{12,8},{9,1... | collective-permute-start | bytes 1769480 | tf_op jit(solution)/shard_map/ppermute | solution.py:444
  10.1 2.0 %collective-permute-done = bf16[128,2304]{1,0:T(8,128)(2,1)S(1)} collective-permute-done((bf16[128,2304]{1,0:T(8,128)(2,1)S(1)}, bf16[128,2304]{1,0:T(8,128)(2,1)S(1)}, u32[]{:S(2)}, u32[]{:S(2)}) %collective-permute-start) | collective-permute-done | bytes 589856 | tf_op jit(solution)/shard_map/ppermute | solution.py:444
  12.0 0.1 add_convert_fusion
  12.2 16.9 %all_to_all.15 = bf16[4,32,2304]{2,1,0:T(8,128)(2,1)S(1)} all-to-all(bf16[4,32,2304]{2,1,0:T(8,128)(2,1)S(1)} %bitcast.3), channel_id=1, replica_groups=mesh['x'=4,'z'=16,'core'=2,'rep'=4] {'x'}, dimensions={0} | all-to-all | bytes 1179648 | tf_op jit(solution)/shard_map/all_to_all | solution.py:405
  29.1 0.1 reduce_sum.24
  29.2 0.1 reshape.15
  29.3 25.5 %all_to_all.16 = bf16[16,2,2304]{2,1,0:T(2,128)(2,1)S(1)} all-to-all(bf16[16,2,2304]{2,1,0:T(2,128)(2,1)S(1)} %reshape.15), channel_id=1, replica_groups=mesh['x'=4,'z'=16,'core'=2,'rep'=4] {'z'}, dimensions={0} | all-to-all | bytes 294912 | tf_op jit(solution)/shard_map/all_to_all | solution.py:405
  54.7 0.1 reduce_sum.25
  54.9 9.7 %all_to_all.17.parts_ref = bf16[4,2,2304]{2,1,0:T(2,128)(2,1)S(1)} all-to-all(bf16[4,2,2304]{2,1,0:T(2,128)(2,1)S(1)} %broadcast_in_dim.3), channel_id=1, replica_groups=mesh['x'=4,'z'=16,'core'=2,'rep'=4] {'rep'}, dimensions={0} | all-to-all | bytes 73728 | tf_op jit(solution)/shard_map/all_to_all | solution.py:405
  64.6 0.7 %finish.1 = (f32[6,192]{1,0:T(8,128)}, f32[6,192]{1,0:T(8,128)}, f32[6,384]{1,0:T(8,128)}) custom-call(bf16[4,2,2304]{2,1,0:T(2,128)(2,1)S(1)} %all_to_all.17.parts_ref), custom_call_target="tpu_custom_call" | custom-call | tf_op jit(solution)/shard_map/finish/pallas_call | solution.py:395
  (1 shorter events, 0.0 us)
Async XLA Ops:
  8.2 3.9 %collective-permute-start = (bf16[128,2304]{1,0:T(8,128)(2,1)S(1)}, bf16[128,2304]{1,0:T(8,128)(2,1)S(1)}, u32[]{:S(2)}, u32[]{:S(2)}) collective-permute-start(bf16[128,2304]{1,0:T(8,128)(2,1)S(1)} %get-tuple-element.12), channel_id=1, source_target_pairs={{0,4},{4,0},{1,5},{5,1},{2,6},{6,2},{3,7},{7,3},{8,12},{12,8},{9,1... | collective-permute-start | bytes 1769480 | tf_op jit(solution)/shard_map/ppermute | solution.py:444
